TPU v7x, 32 devices: a whole 2x2x4 slice. The times are simulated.
32 devices in a mesh: seq: 8 (over z, x), head: 4 (over y, core).
Axes of the slice: x: 2, y: 2, z: 4, core: 2. Of those that a mesh axis runs over, the one named last changes fastest.
Arguments:
- queries: bfloat16 [9216, 32, 128], P(('seq', 'head')), may hold values from -4 to 4
- key_states: bfloat16 [9216, 4, 128], P(('seq', 'head')), may hold values from -4 to 4
- value_states: bfloat16 [9216, 4, 128], P(('seq', 'head')), may hold values from -6 to 6
- outputs: bfloat16 [9216, 32, 128], P(('seq', 'head')), may hold values from -6 to 6
- output_grad: bfloat16 [9216, 32, 128], P(('seq', 'head')), may hold values from -96 to 96
- logsumexp: float32 [9216, 32], P(('seq', 'head')), may hold values from 6.8 to 7.8
- random_owner: int32 [72, 3], replicated, may hold values from 0 to 7, all different within a row; in each aligned block of 9 rows (0 to 8, 9 to 17, ...) at most 4 rows name the same one
- random_slot: int32 [72, 3], replicated, may hold values from 0 to 8
Outputs:
- query_grad: bfloat16 [9216, 32, 128], P(('seq', 'head'))
- key_grad: bfloat16 [9216, 4, 128], P(('seq', 'head'))
- value_grad: bfloat16 [9216, 4, 128], P(('seq', 'head'))
Inputs may be any that keep to these rules, and one draw needn't show every extreme that they name: `random_owner`: each row names 3 different indices. Within the 9 rows of one index of seq (aligned blocks of 9 rows), no index of seq appears more than 4 times, and some index appears exactly 4 times in some block.
All inputs are finite; a program needn't handle non-finite values.
Results may differ from a plain program's by a relative error of at most 0.005.
Values may be sent and summed in bfloat16 or wider, within the bound.
A program may use at most 128 MiB of HBM per device.

v0:
```python
import jax
import jax.numpy as jnp
from jax import lax
from jax.sharding import PartitionSpec as P

HD = 128
BLK = 128
G = 2
RND = 3


def extended_2(value, sides, width):
    for axis, dim in sides:
        devices, length = (lax.axis_size(axis), value.shape[dim])
        up = [(i, (i + 1) % devices) for i in range(devices - 1)]
        down = [(j, i) for i, j in up]
        last = lax.slice_in_dim(value, length - width, length, axis=dim)
        leading = lax.slice_in_dim(value, 0, width, axis=dim)
        before = lax.ppermute(last, axis, up)
        after = lax.ppermute(leading, axis, down)
        value = jnp.concatenate([before, value, after], axis=dim)
    return value


def broadcast(value, axis, source):
    kept = jnp.where(lax.axis_index(axis) == source, value, 0).astype(value.dtype)
    return lax.psum(kept, axis)


def from_behind(value, axis, steps):
    count = lax.axis_size(axis)
    leading, last = (max(0, -steps), min(count, count - steps))
    return lax.ppermute(value, axis, [(source, source + steps) for source in range(leading, last)])


def block_grads(
    query_block, grad_block, logsum_block, delta_block, key_blocks, value_blocks, validity
):
    scaling = 1.0 / HD**0.5
    scores = (
        jnp.einsum("ighd,mjgd->mghij", query_block, key_blocks, preferred_element_type=jnp.float32)
        * scaling
    )
    weights = (
        jnp.exp(scores - jnp.transpose(logsum_block, (1, 2, 0))[None, :, :, :, None])
        * validity[:, None, None, None, None]
    )
    weights_rounded = weights.astype(jnp.bfloat16)
    weight_grad = jnp.einsum(
        "ighd,mjgd->mghij", grad_block, value_blocks, preferred_element_type=jnp.float32
    )
    score_grad = (
        weights * (weight_grad - jnp.transpose(delta_block, (1, 2, 0))[None, :, :, :, None])
    ).astype(jnp.bfloat16)
    query_part = (
        jnp.einsum("mghij,mjgd->ighd", score_grad, key_blocks, preferred_element_type=jnp.float32)
        * scaling
    )
    key_part = (
        jnp.einsum("mghij,ighd->mjgd", score_grad, query_block, preferred_element_type=jnp.float32)
        * scaling
    )
    value_part = jnp.einsum(
        "mghij,ighd->mjgd", weights_rounded, grad_block, preferred_element_type=jnp.float32
    )
    return (query_part, jnp.stack([key_part, value_part], axis=2))


def local_grads(query_split, grad_split, logsum_split, delta_split, chosen_kv, validity):

    def single_block(items):
        return block_grads(*items)

    return lax.map(
        single_block,
        (
            query_split,
            grad_split,
            logsum_split,
            delta_split,
            chosen_kv[:, :, :, 0],
            chosen_kv[:, :, :, 1],
            validity,
        ),
    )


def pair_lists(block_ids, owners, slots, blocks_local, block_count):
    window_ids = block_ids[:, None] + jnp.arange(-1, 2, dtype=jnp.int32)[None, :]
    random_ids = owners * blocks_local + slots
    window_ok = (window_ids >= G) & (window_ids <= block_count - 1)
    random_ok = (random_ids >= G) & (jnp.abs(random_ids - block_ids[:, None]) >= 2)
    validity = jnp.concatenate(
        [
            jnp.ones((block_ids.shape[0], G), jnp.float32),
            window_ok.astype(jnp.float32),
            random_ok.astype(jnp.float32),
        ],
        axis=1,
    )
    return (window_ids, random_ids, validity)


def per_device(
    queries, key_states, value_states, outputs, output_grad, logsumexp, random_owner, random_slot
):
    delta_seq = jnp.einsum("thd,thd->th", output_grad, outputs, preferred_element_type=jnp.float32)
    query_loc, key_loc, value_loc, grad_loc = (
        lax.all_to_all(queries, "head", split_axis=1, concat_axis=0, tiled=True),
        lax.all_to_all(key_states, "head", split_axis=1, concat_axis=0, tiled=True),
        lax.all_to_all(value_states, "head", split_axis=1, concat_axis=0, tiled=True),
        lax.all_to_all(output_grad, "head", split_axis=1, concat_axis=0, tiled=True),
    )
    logsum_loc, delta_loc = (
        lax.all_to_all(logsumexp, "head", split_axis=1, concat_axis=0, tiled=True),
        lax.all_to_all(delta_seq, "head", split_axis=1, concat_axis=0, tiled=True),
    )
    tok_count = query_loc.shape[0]
    heads_local = query_loc.shape[1]
    kv_heads = key_loc.shape[1]
    group = heads_local // kv_heads
    blocks_local = tok_count // BLK
    seq_count = lax.axis_size("seq")
    seq_index = lax.axis_index("seq")
    block_count = seq_count * blocks_local
    rows_each = blocks_local * RND
    most_slots = max(1, (rows_each + seq_count - 1) // seq_count)
    query_split = query_loc.reshape(blocks_local, BLK, kv_heads, group, HD)
    grad_split = grad_loc.reshape(blocks_local, BLK, kv_heads, group, HD)
    logsum_split = logsum_loc.reshape(blocks_local, BLK, kv_heads, group)
    delta_split = delta_loc.reshape(blocks_local, BLK, kv_heads, group)
    kv_loc = jnp.stack([key_loc, value_loc], axis=1)
    kv_blocks = kv_loc.reshape(blocks_local, BLK, 2, kv_heads, HD)
    block_ids = seq_index * blocks_local + jnp.arange(blocks_local, dtype=jnp.int32)
    my_owner = lax.dynamic_slice_in_dim(random_owner, seq_index * blocks_local, blocks_local, 0)
    my_slot = lax.dynamic_slice_in_dim(random_slot, seq_index * blocks_local, blocks_local, 0)
    window_ids, random_ids, validity = pair_lists(
        block_ids, my_owner, my_slot, blocks_local, block_count
    )
    owner_table = random_owner.reshape(seq_count, rows_each)
    slot_table = random_slot.reshape(seq_count, rows_each)
    entry_pos = jnp.arange(rows_each, dtype=jnp.int32)
    before_mask = entry_pos[None, :] < entry_pos[:, None]
    same_owner = owner_table[:, :, None] == owner_table[:, None, :]
    rank_table = jnp.sum((same_owner & before_mask[None, :, :]).astype(jnp.int32), axis=2)
    my_rank = lax.dynamic_slice_in_dim(rank_table, seq_index, 1, 0).reshape(blocks_local, RND)
    slot_ids = jnp.arange(most_slots, dtype=jnp.int32)
    local_ids = jnp.arange(blocks_local, dtype=jnp.int32)
    local_hits = (
        (owner_table == seq_index)[:, :, None, None]
        & (rank_table[:, :, None, None] == slot_ids[None, None, :, None])
        & (slot_table[:, :, None, None] == local_ids[None, None, None, :])
    )
    selector = jnp.sum(local_hits.astype(jnp.float32), axis=1)
    extended = extended_2(kv_loc, (("seq", 0),), BLK)
    ext_blocks = extended.reshape(blocks_local + 2, BLK, 2, kv_heads, HD)
    window_kv = jnp.stack(
        [ext_blocks[offset : offset + blocks_local] for offset in range(3)], axis=1
    )
    global_kv = broadcast(kv_loc[: G * BLK], "seq", 0).reshape(G, BLK, 2, kv_heads, HD)
    outgoing = jnp.einsum(
        "pml,lbtgd->pmbtgd",
        selector.astype(jnp.bfloat16),
        kv_blocks,
        preferred_element_type=jnp.float32,
    ).astype(jnp.bfloat16)
    fetched = lax.all_to_all(outgoing, "seq", split_axis=0, concat_axis=0, tiled=True)
    random_kv = fetched[my_owner, my_rank]
    global_wide = jnp.broadcast_to(global_kv[None], (blocks_local,) + global_kv.shape)
    chosen = jnp.concatenate([global_wide, window_kv, random_kv], axis=1)
    query_part, kv_part = local_grads(
        query_split, grad_split, logsum_split, delta_split, chosen, validity
    )
    global_part = jnp.sum(kv_part[:, :G], axis=0)
    window_part = kv_part[:, G : G + 3]
    random_part = kv_part[:, G + 3 :]
    global_total = lax.psum(global_part, "seq")
    padded_parts = [
        jnp.pad(window_part[:, offset], ((offset, 2 - offset), (0, 0), (0, 0), (0, 0), (0, 0)))
        for offset in range(3)
    ]
    ext_grad = padded_parts[0] + padded_parts[1] + padded_parts[2]
    own_grad = ext_grad[1 : blocks_local + 1]
    flat_target = (my_owner * most_slots + my_rank).reshape(-1)
    owner_onehot = (
        flat_target[None, :] == jnp.arange(seq_count * most_slots, dtype=jnp.int32)[:, None]
    ).astype(jnp.float32)
    returning = jnp.dot(
        owner_onehot,
        random_part.reshape(rows_each, -1),
        precision=lax.Precision.HIGHEST,
        preferred_element_type=jnp.float32,
    )
    returning = returning.reshape(seq_count, most_slots, BLK, 2, kv_heads, HD)
    from_upper = from_behind(ext_grad[0].astype(jnp.bfloat16), "seq", -1).astype(jnp.float32)
    from_lower = from_behind(ext_grad[blocks_local + 1].astype(jnp.bfloat16), "seq", 1).astype(
        jnp.float32
    )
    returned = lax.all_to_all(returning, "seq", split_axis=0, concat_axis=0, tiled=True)
    own_grad = own_grad.at[blocks_local - 1].add(from_upper)
    own_grad = own_grad.at[0].add(from_lower)
    own_grad = own_grad + jnp.einsum(
        "pml,pmbtgd->lbtgd",
        selector,
        returned,
        precision=lax.Precision.HIGHEST,
        preferred_element_type=jnp.float32,
    )
    global_here = jnp.where(seq_index == 0, global_total, jnp.zeros_like(global_total))
    own_grad = own_grad.at[:G].add(global_here)
    kv_grad = own_grad.reshape(tok_count, 2, kv_heads, HD)
    query_grad_loc = query_part.reshape(tok_count, heads_local, HD).astype(jnp.bfloat16)
    key_grad_loc = kv_grad[:, 0].astype(jnp.bfloat16)
    value_grad_loc = kv_grad[:, 1].astype(jnp.bfloat16)
    query_grad, key_grad, value_grad = (
        lax.all_to_all(query_grad_loc, "head", split_axis=0, concat_axis=1, tiled=True),
        lax.all_to_all(key_grad_loc, "head", split_axis=0, concat_axis=1, tiled=True),
        lax.all_to_all(value_grad_loc, "head", split_axis=0, concat_axis=1, tiled=True),
    )
    return (query_grad, key_grad, value_grad)


def solution(mesh):
    placed = (
        P(("seq", "head"), None, None),
        P(("seq", "head"), None, None),
        P(("seq", "head"), None, None),
        P(("seq", "head"), None, None),
        P(("seq", "head"), None, None),
        P(("seq", "head"), None),
        P(),
        P(),
    )
    return jax.shard_map(
        per_device,
        mesh=mesh,
        in_specs=placed,
        out_specs=(
            P(("seq", "head"), None, None),
            P(("seq", "head"), None, None),
            P(("seq", "head"), None, None),
        ),
        check_vma=False,
    )
```

profile of v0, /device:TPU:0, one launch (start us, length us, event | category | flops | bytes accessed | tf_op | source)
XLA Modules:
  0.0 552.0 jit_solution(14091224354696129399)
XLA Ops:
  7.2 4.3 all-to-all-start.4
  27.5 5.6 %all-to-all-done.1 = bf16[288,4,128]{2,0,1:T(8,128)(2,1)S(1)} async-done(((bf16[288,4,128]{2,0,1:T(8,128)(2,1)}), bf16[288,4,128]{2,0,1:T(8,128)(2,1)S(1)}, u32[]{:S(2)}, u32[]{:S(2)}) %all-to-all-start.1) | async-done | bytes 294944 | tf_op jit(solution)/shard_map/all_to_all | solution.py:111
  42.8 4.5 all-to-all-start.3
  49.7 26.2 %all-to-all-done.3 = bf16[288,32,128]{2,0,1:T(8,128)(2,1)} async-done(((bf16[288,32,128]{2,0,1:T(8,128)(2,1)}), bf16[288,32,128]{2,0,1:T(8,128)(2,1)}, u32[]{:S(2)}, u32[]{:S(2)}) %all-to-all-start.3) | async-done | bytes 2359328 | tf_op jit(solution)/shard_map/all_to_all | solution.py:109
  85.6 22.4 %all-to-all-done.5 = bf16[288,32,128]{2,0,1:T(8,128)(2,1)S(1)} async-done(((bf16[288,32,128]{2,0,1:T(8,128)(2,1)}), bf16[288,32,128]{2,0,1:T(8,128)(2,1)S(1)}, u32[]{:S(2)}, u32[]{:S(2)}) %all-to-all-start.5) | async-done | bytes 2359328 | tf_op jit(solution)/shard_map/all_to_all | solution.py:112
  108.0 6.3 %all-to-all-start.2 = ((bf16[8,4,128,2,1,128]{5,3,2,1,4,0:T(2,128)(2,1)}), bf16[8,4,128,2,1,128]{5,3,2,1,4,0:T(2,128)(2,1)}, u32[]{:S(2)}, u32[]{:S(2)}) async-start(bf16[8,4,128,2,1,128]{5,3,2,1,4,0:T(2,128)(2,1)} %copy.262), calls=%async_computation.2 | async-start | bytes 4194304 | tf_op jit(solution)/shard_map/all_to_all | solution.py:167
  119.0 5.6 %collective-permute-start = (bf16[128,2,1,128]{3,0,2,1:T(8,128)(2,1)S(1)}, bf16[128,2,1,128]{3,0,2,1:T(8,128)(2,1)}, u32[]{:S(2)}, u32[]{:S(2)}) collective-permute-start(bf16[128,2,1,128]{3,0,2,1:T(8,128)(2,1)S(1)} %get-tuple-element.197), channel_id=1, source_target_pairs={{0,4},{4,8},{8,12},{12,16},{16,20},{20,24},{24,28},{1,5},{5,9},{9,... | collective-permute-start | bytes 196616 | tf_op jit(solution)/shard_map/ppermute | solution.py:19
  125.4 4.2 collective-permute-done.1
  130.2 4.0 collective-permute-done
  136.1 70.3 %all-reduce.6.cloned.1.call-done = bf16[2,128,2,128]{3,1,0,2:T(8,128)(2,1)} async-done(((bf16[2,128,2,128]{3,1,0,2:T(8,128)(2,1)}), bf16[2,128,2,128]{3,1,0,2:T(8,128)(2,1)}) %all-reduce.6.cloned.1.call-update) | async-done | bytes 131088 | tf_op jit(solution)/shard_map/psum | solution.py:27
  226.3 6.4 %slice_bitcast_fusion = (bf16[9,8,128,1,128]{4,2,1,3,0:T(8,128)(2,1)}, bf16[9,8,128,1,128]{4,2,1,3,0:T(8,128)(2,1)}) fusion(bf16[9,8,128,2,1,128]{5,2,4,3,1,0:T(8,128)(2,1)} %constant_dynamic-update-slice_fusion.1), kind=kLoop, calls=%fused_computation.51 | loop fusion | bytes 9437184 | tf_op jit(solution)/shard_map/while | solution.py:74
  232.7 122.5 %while.15 = (s32[]{:T(128)}, bf16[9,128,1,8,128]{4,3,1,0,2:T(8,128)(2,1)}, f32[9,8,128,2,1,128]{2,5,1,3,4,0:T(8,128)}, bf16[9,8,128,1,128]{4,2,1,3,0:T(8,128)(2,...) while((s32[]{:T(128)}, ...), condition=%wide.region_4.5_spmd, body=%wide.region_3.4_spmd.sunk | while | flops 1353318400 | bytes 43020592 | solution.py:74
  357.4 4.8 copy.294
  362.2 6.2 %reshape.411 = f32[27,32768]{1,0:T(8,128)} reshape(f32[9,3,128,2,1,128]{5,3,2,1,0,4:T(2,128)} %copy.294) | data formatting | bytes 7077888 | tf_op jit(solution)/shard_map/reshape | solution.py:190
  368.4 4.9 reshape.412
  373.3 4.4 fusion.53
  377.7 4.2 copy.296
  381.9 4.6 all-to-all-start.8
  386.6 9.6 %copy.287 = f32[9,8,128,2,1,128]{5,2,3,0,4,1:T(8,128)} copy(f32[9,8,128,2,1,128]{2,5,1,3,4,0:T(8,128)} %get-tuple-element.93) | data formatting | bytes 18874368 | tf_op jit(solution)/shard_map/while | solution.py:74
  402.6 5.2 collective-permute-start.3
  408.6 74.4 %all-to-all-done.8 = f32[8,4,128,2,1,128]{5,3,2,1,4,0:T(2,128)} async-done(((f32[8,4,128,2,1,128]{5,3,2,1,4,0:T(2,128)}), f32[8,4,128,2,1,128]{5,3,2,1,4,0:T(2,128)}, u32[]{:S(2)}, u32[]{:S(2)}) %all-to-all-start.8) | async-done | bytes 4194336 | tf_op jit(solution)/shard_map/all_to_all | solution.py:199
  488.8 11.4 %fusion.56 = f32[9,128,2,128]{3,0,2,1:T(8,128)S(1)} fusion(f32[8,4,128,2,1,128]{5,3,2,1,4,0:T(2,128)} %all-to-all-done.8, f32[8,4,9]{0,2,1:T(8,128)S(1)} %copy-done.5), kind=kOutput, calls=%fused_computation.58 | convolution fusion | flops 113246208 | bytes 5375104 | tf_op jit(solution)/shard_map/pml,pmbtgd->lbtgd/dot_general | solution.py:202
  500.9 19.8 %all-reduce.8.cloned.1.call-done = f32[2,128,2,1,128]{4,1,3,2,0:T(8,128)} async-done(((f32[2,128,2,1,128]{4,1,3,2,0:T(8,128)}), f32[2,128,2,1,128]{4,1,3,2,0:T(8,128)}) %all-reduce.8.cloned.1.call-update) | async-done | bytes 262160 | tf_op jit(solution)/shard_map/psum | solution.py:177
  529.2 4.7 all-to-all-done.9
  (247 shorter events, 222.6 us)
Async XLA Ops:
  7.2 8.8 %all-to-all-start.4 = ((f32[288,4,8]{0,2,1:T(8,128)}), f32[288,4,8]{0,2,1:T(8,128)S(1)}, u32[]{:S(2)}, u32[]{:S(2)}) async-start(f32[288,4,8]{0,2,1:T(8,128)} %bitcast.356), calls=%async_computation.4 | async-start | bytes 98304 | tf_op jit(solution)/shard_map/all_to_all | solution.py:115
  11.4 7.8 %copy-start.6 = (bf16[288,4,128]{2,1,0:T(4,128)(2,1)S(1)}, bf16[288,4,128]{2,1,0:T(4,128)(2,1)}, u32[]{:S(2)}) copy-start(bf16[288,4,128]{2,1,0:T(4,128)(2,1)} %param.18) | copy-start | bytes 884740
  11.4 15.3 %copy-start.7 = (bf16[288,4,128]{2,1,0:T(4,128)(2,1)S(1)}, bf16[288,4,128]{2,1,0:T(4,128)(2,1)}, u32[]{:S(2)}) copy-start(bf16[288,4,128]{2,1,0:T(4,128)(2,1)} %param.17) | copy-start | bytes 884740
  15.2 21.3 %copy-start.3 = (bf16[288,32,128]{2,1,0:T(8,128)(2,1)S(1)}, bf16[288,32,128]{2,1,0:T(8,128)(2,1)}, u32[]{:S(2)}) copy-start(bf16[288,32,128]{2,1,0:T(8,128)(2,1)} %param.16) | copy-start | bytes 7077892
  15.9 7.3 %all-to-all-start.6 = ((f32[288,4,8]{0,2,1:T(8,128)}), f32[288,4,8]{0,2,1:T(8,128)S(1)}, u32[]{:S(2)}, u32[]{:S(2)}) async-start(f32[288,4,8]{0,2,1:T(8,128)} %bitcast.81), calls=%async_computation.6 | async-start | bytes 98304 | tf_op jit(solution)/shard_map/all_to_all | solution.py:116
  23.3 9.8 %all-to-all-start.1 = ((bf16[288,4,128]{2,0,1:T(8,128)(2,1)}), bf16[288,4,128]{2,0,1:T(8,128)(2,1)S(1)}, u32[]{:S(2)}, u32[]{:S(2)}) async-start(bf16[288,4,128]{2,0,1:T(8,128)(2,1)} %copy.251), calls=%async_computation.1 | async-start | bytes 589824 | tf_op jit(solution)/shard_map/all_to_all | solution.py:111
  33.0 9.8 %all-to-all-start = ((bf16[288,4,128]{2,0,1:T(8,128)(2,1)}), bf16[288,4,128]{2,0,1:T(8,128)(2,1)S(1)}, u32[]{:S(2)}, u32[]{:S(2)}) async-start(bf16[288,4,128]{2,0,1:T(8,128)(2,1)} %copy.250), calls=%async_computation | async-start | bytes 589824 | tf_op jit(solution)/shard_map/all_to_all | solution.py:110
  38.8 8.5 %copy-start.1 = (bf16[288,32,128]{2,1,0:T(8,128)(2,1)S(1)}, bf16[288,32,128]{2,1,0:T(8,128)(2,1)}, u32[]{:S(2)}) copy-start(bf16[288,32,128]{2,1,0:T(8,128)(2,1)} %param.20) | copy-start | bytes 7077892
  42.8 33.1 %all-to-all-start.3 = ((bf16[288,32,128]{2,0,1:T(8,128)(2,1)}), bf16[288,32,128]{2,0,1:T(8,128)(2,1)}, u32[]{:S(2)}, u32[]{:S(2)}) async-start(bf16[288,32,128]{2,0,1:T(8,128)(2,1)} %copy.270), calls=%async_computation.3 | async-start | bytes 4718592 | tf_op jit(solution)/shard_map/all_to_all | solution.py:109
  49.7 29.8 %copy-start.10 = (s32[72,3]{0,1:T(4,128)S(1)}, s32[72,3]{0,1:T(4,128)}, u32[]{:S(2)}) copy-start(s32[72,3]{0,1:T(4,128)} %param.23) | copy-start | bytes 2596
  49.7 30.0 %copy-start.9 = (s32[72,3]{0,1:T(4,128)S(1)}, s32[72,3]{0,1:T(4,128)}, u32[]{:S(2)}) copy-start(s32[72,3]{0,1:T(4,128)} %param.22) | copy-start | bytes 2596
  75.9 32.1 %all-to-all-start.5 = ((bf16[288,32,128]{2,0,1:T(8,128)(2,1)}), bf16[288,32,128]{2,0,1:T(8,128)(2,1)S(1)}, u32[]{:S(2)}, u32[]{:S(2)}) async-start(bf16[288,32,128]{2,0,1:T(8,128)(2,1)} %copy.274), calls=%async_computation.5 | async-start | bytes 4718592 | tf_op jit(solution)/shard_map/all_to_all | solution.py:112
  108.0 110.9 %all-to-all-start.2 = ((bf16[8,4,128,2,1,128]{5,3,2,1,4,0:T(2,128)(2,1)}), bf16[8,4,128,2,1,128]{5,3,2,1,4,0:T(2,128)(2,1)}, u32[]{:S(2)}, u32[]{:S(2)}) async-start(bf16[8,4,128,2,1,128]{5,3,2,1,4,0:T(2,128)(2,1)} %copy.262), calls=%async_computation.2 | async-start | bytes 4194304 | tf_op jit(solution)/shard_map/all_to_all | solution.py:167
  114.2 92.2 %all-reduce.6.cloned.1.call-start = ((), (), s32[]{:S(2)}) async-start(), calls=%async_computation.11 | async-start | bytes 262144 | tf_op jit(solution)/shard_map/psum | solution.py:27
  117.7 11.9 %collective-permute-start.1 = (bf16[128,2,1,128]{3,0,2,1:T(8,128)(2,1)S(1)}, bf16[128,2,1,128]{3,0,2,1:T(8,128)(2,1)S(1)}, u32[]{:S(2)}, u32[]{:S(2)}) collective-permute-start(bf16[128,2,1,128]{3,0,2,1:T(8,128)(2,1)S(1)} %get-tuple-element.196), channel_id=1, source_target_pairs={{4,0},{8,4},{12,8},{16,12},{20,16},{24,20},{28,24},{5,1},{9,5},{13... | collective-permute-start | bytes 196616 | tf_op jit(solution)/shard_map/ppermute | solution.py:20
  119.0 15.2 %collective-permute-start = (bf16[128,2,1,128]{3,0,2,1:T(8,128)(2,1)S(1)}, bf16[128,2,1,128]{3,0,2,1:T(8,128)(2,1)}, u32[]{:S(2)}, u32[]{:S(2)}) collective-permute-start(bf16[128,2,1,128]{3,0,2,1:T(8,128)(2,1)S(1)} %get-tuple-element.197), channel_id=1, source_target_pairs={{0,4},{4,8},{8,12},{12,16},{16,20},{20,24},{24,28},{1,5},{5,9},{9,... | collective-permute-start | bytes 196616 | tf_op jit(solution)/shard_map/ppermute | solution.py:19
  368.4 4.9 copy-start.11
  381.9 101.1 %all-to-all-start.8 = ((f32[8,4,128,2,1,128]{5,3,2,1,4,0:T(2,128)}), f32[8,4,128,2,1,128]{5,3,2,1,4,0:T(2,128)}, u32[]{:S(2)}, u32[]{:S(2)}) async-start(f32[8,4,128,2,1,128]{5,3,2,1,4,0:T(2,128)} %copy.296), calls=%async_computation.8 | async-start | bytes 8388608 | tf_op jit(solution)/shard_map/all_to_all | solution.py:199
  386.5 134.2 %all-reduce.8.cloned.1.call-start = ((), (), s32[]{:S(2)}) async-start(), calls=%async_computation.12 | async-start | bytes 524288 | tf_op jit(solution)/shard_map/psum | solution.py:177
  399.4 87.5 %collective-permute-start.2 = (bf16[128,2,1,128]{3,0,1,2:T(8,128)(2,1)}, bf16[128,2,1,128]{3,0,1,2:T(8,128)(2,1)}, u32[]{:S(2)}, u32[]{:S(2)}) collective-permute-start(bf16[128,2,1,128]{3,0,1,2:T(8,128)(2,1)} %get-tuple-element.191), channel_id=1, source_target_pairs={{4,0},{8,4},{12,8},{16,12},{20,16},{24,20},{28,24},{5,1},{9,5},{13... | collective-permute-start | bytes 196616 | tf_op jit(solution)/shard_map/ppermute | solution.py:33
  402.6 85.4 %collective-permute-start.3 = (bf16[128,2,1,128]{3,0,1,2:T(8,128)(2,1)}, bf16[128,2,1,128]{3,0,1,2:T(8,128)(2,1)}, u32[]{:S(2)}, u32[]{:S(2)}) collective-permute-start(bf16[128,2,1,128]{3,0,1,2:T(8,128)(2,1)} %get-tuple-element.190), channel_id=1, source_target_pairs={{0,4},{4,8},{8,12},{12,16},{16,20},{20,24},{24,28},{1,5},{5,9},{9,... | collective-permute-start | bytes 196616 | tf_op jit(solution)/shard_map/ppermute | solution.py:33
  483.1 41.1 %all-to-all-start.7 = ((bf16[1152,8,128]{2,1,0:T(8,128)(2,1)}), bf16[1152,8,128]{2,1,0:T(8,128)(2,1)S(1)}, u32[]{:S(2)}, u32[]{:S(2)}) async-start(bf16[1152,8,128]{2,1,0:T(8,128)(2,1)} %bitcast.342), calls=%async_computation.7 | async-start | bytes 4718592 | tf_op jit(solution)/shard_map/all_to_all | solution.py:216
  524.1 9.8 %all-to-all-start.9 = ((bf16[4,2,18432]{2,1,0:T(2,128)(2,1)}), bf16[4,2,18432]{2,1,0:T(2,128)(2,1)S(1)}, u32[]{:S(2)}, u32[]{:S(2)}) async-start(bf16[4,2,18432]{2,1,0:T(2,128)(2,1)} %reshape.453), calls=%async_computation.9 | async-start | bytes 589824 | tf_op jit(solution)/shard_map/all_to_all | solution.py:217
  533.9 9.8 %all-to-all-start.10 = ((bf16[4,2,18432]{2,1,0:T(2,128)(2,1)}), bf16[4,2,18432]{2,1,0:T(2,128)(2,1)S(1)}, u32[]{:S(2)}, u32[]{:S(2)}) async-start(bf16[4,2,18432]{2,1,0:T(2,128)(2,1)} %reshape.455), calls=%async_computation.10 | async-start | bytes 589824 | tf_op jit(solution)/shard_map/all_to_all | solution.py:218
  (13 other events, 37.7 us)
Sparse Core Ops, SparseCore 0:
  125.5 80.9 all-reduce.5
  408.7 111.9 all-reduce.7
where the time goes:
time: 562 us; the launch traced here: 552 us
  waiting for transfers between devices  242 us (43%)
  local copies, waits for them, and re-layouts  108 us (19%)
  matrix products  103 us (18%)
  starting transfers between devices  57.7 us (10%)
  other arithmetic  25.4 us (5%)
  between operations  14.8 us (3%)
    all_to_all x1, waiting for transfers between devices, per_device(): lax.all_to_all(returning, 'seq', split_axis=0, concat_axis=0, tiled=True)  74.4 us
    psum x1, waiting for transfers between devices, broadcast(): return lax.psum(kept, axis)  70.3 us
    dot_general x9, matrix products, block_grads(): jnp.einsum('mghij,ighd->mjgd', weights_rounded, grad_block, preferred_ele...  29.3 us
    all_to_all x1, waiting for transfers between devices, per_device(): lax.all_to_all(queries, 'head', split_axis=1, concat_axis=0, tiled=True)  26.2 us
    all_to_all x1, waiting for transfers between devices, per_device(): lax.all_to_all(output_grad, 'head', split_axis=1, concat_axis=0, tiled=True)  22.4 us
    dot_general x9, matrix products, block_grads(): jnp.einsum('ighd,mjgd->mghij', grad_block, value_blocks, preferred_elemen...  21.9 us
    psum x1, waiting for transfers between devices, per_device(): global_total = lax.psum(global_part, 'seq')  19.8 us
    dynamic_slice x18, local copies, waits for them, and re-layouts, local_grads(): lax.map(single_block, (query_split, grad_split, logsum_split, delta_split...  17.3 us
  transfers between devices with their start and end apart: 17, of which 12 were waited for; matrix products, arithmetic and copies ran while one was open for 13% of the time, Pallas kernels for 0%

commit v1 on v0

v1 whole, which is shorter than its diff:
```python
import functools
import math

import jax
import jax.numpy as jnp
from jax import lax
from jax.experimental import pallas as pl
from jax.experimental.pallas import tpu as pltpu
from jax.sharding import PartitionSpec as P

HD = 128
BLK = 128
G = 2
RND = 3
MESH = pl.DeviceIdType.MESH
F32 = jnp.float32
BF16 = jnp.bfloat16
LOG2E = math.log2(math.e)


def greet(n_seq, n_head, seq, head):
    barrier = pltpu.get_barrier_semaphore()

    def to_head(d, c):
        pl.semaphore_signal(
            barrier, inc=1, device_id={"head": lax.rem(head + d, n_head)}, device_id_type=MESH
        )
        return c

    def to_seq(d, c):
        pl.semaphore_signal(
            barrier, inc=1, device_id={"seq": lax.rem(seq + d, n_seq)}, device_id_type=MESH
        )
        return c

    lax.fori_loop(1, n_head, to_head, 0)
    lax.fori_loop(1, n_seq, to_seq, 0)
    pl.semaphore_wait(barrier, n_head + n_seq - 2)


def remote(src, dst, send, recv, **where):
    return pltpu.make_async_remote_copy(
        src_ref=src,
        dst_ref=dst,
        send_sem=send,
        recv_sem=recv,
        device_id=where,
        device_id_type=MESH,
    )


def exchange_in(
    n_seq, n_head, most,
    pick, q_in, g_in, kv_in, ld_in,
    q_out, g_out, ld_out, kv_out, glob_out, rand_out,
    picked, held, hs, hr, ls, ss, sr, ns, nr, gs, gr,
):
    seq, head = lax.axis_index("seq"), lax.axis_index("head")
    rows = q_in.shape[1]
    toks = kv_in.shape[2]
    span = n_head * toks
    greet(n_seq, n_head, seq, head)

    q_to = q_out.at[pl.ds(pl.multiple_of(head * rows, rows), rows), :]
    g_to = g_out.at[pl.ds(pl.multiple_of(head * rows, rows), rows), :]
    kv_to = kv_out.at[:, pl.ds(pl.multiple_of(BLK + head * toks, 32), toks), :]
    ld_to = ld_out.at[head]

    def head_copy(kind, d):
        peer = lax.rem(head + d, n_head)
        src, dst = (
            (kv_in.at[peer], kv_to),
            (ld_in.at[peer], ld_to),
            (q_in.at[peer], q_to),
            (g_in.at[peer], g_to),
        )[kind]
        return remote(src, dst, hs.at[kind, d], hr.at[kind, d], head=peer)

    own = [
        pltpu.make_async_copy(kv_in.at[head], kv_to, ls.at[0]),
        pltpu.make_async_copy(ld_in.at[head], ld_to, ls.at[1]),
        pltpu.make_async_copy(q_in.at[head], q_to, ls.at[2]),
        pltpu.make_async_copy(g_in.at[head], g_to, ls.at[3]),
    ]
    for kind in range(4):
        for d in range(1, n_head):
            head_copy(kind, d).start()
        own[kind].start()
    own[0].wait()
    for d in range(1, n_head):
        head_copy(0, d).wait_recv()

    up, down = lax.rem(seq + 1, n_seq), lax.rem(seq + n_seq - 1, n_seq)
    to_up = remote(
        kv_out.at[:, pl.ds(span, BLK), :], kv_out.at[:, pl.ds(0, BLK), :],
        ns.at[0], nr.at[0], seq=up,
    )
    to_down = remote(
        kv_out.at[:, pl.ds(BLK, BLK), :], kv_out.at[:, pl.ds(BLK + span, BLK), :],
        ns.at[1], nr.at[1], seq=down,
    )

    def rand_copy(d):
        peer = lax.rem(seq + d, n_seq)
        return remote(picked.at[peer], rand_out.at[seq], ss.at[d], sr.at[d], seq=peer)

    def glob_copy(d):
        return remote(
            kv_out.at[:, pl.ds(BLK, G * BLK), :], glob_out, gs.at[d], gr, seq=d
        )

    def fill(d, c):
        peer = lax.rem(seq + d, n_seq)
        for m in range(most):
            picked[peer, m] = held[pick[peer * most + m]]
        return c

    def start(d, c):
        rand_copy(d).start()
        return c

    def finish(d, c):
        rand_copy(d).wait()
        return c

    for block in range(span // BLK):
        held[block] = kv_out[:, (block + 1) * BLK : (block + 2) * BLK, :]
    lax.fori_loop(0, n_seq, fill, 0)
    to_up.start()
    to_down.start()

    @pl.when(seq == 0)
    def _():
        def go(d, c):
            glob_copy(d).start()
            return c

        lax.fori_loop(1, n_seq, go, 0)
        glob_out[...] = kv_out[:, BLK : BLK + G * BLK, :]

    lax.fori_loop(1, n_seq, start, 0)
    rand_out[seq] = picked[seq]
    for kind in range(1, 4):
        own[kind].wait()
        for d in range(1, n_head):
            head_copy(kind, d).wait_recv()
    for kind in range(4):
        for d in range(1, n_head):
            head_copy(kind, d).wait_send()
    to_up.wait()
    to_down.wait()

    @pl.when(seq == 0)
    def _():
        def done(d, c):
            glob_copy(d).wait_send()
            return c

        lax.fori_loop(1, n_seq, done, 0)

    @pl.when(seq > 0)
    def _():
        glob_copy(0).wait_recv()

    lax.fori_loop(1, n_seq, finish, 0)


def dot(a, b, ca, cb):
    return lax.dot_general(a, b, (((ca,), (cb,)), ((), ())), preferred_element_type=F32)


def attend(
    blocks, pos, bias,
    q_ref, g_ref, ld_ref, kv_ref, glob_ref, rand_ref,
    dq_ref, own_ref, halo_ref, gpart_ref, rpart_ref,
    kcat, vcat, acc, gacc,
):
    b = pl.program_id(0)
    scaling = 1.0 / HD**0.5

    @pl.when(b == 0)
    def _():
        acc[...] = jnp.zeros_like(acc)
        gacc[...] = jnp.zeros_like(gacc)
        rpart_ref[...] = jnp.zeros_like(rpart_ref)

    at = pl.multiple_of(b * BLK, BLK)
    win = pl.ds(at, 3 * BLK)
    first = G * BLK
    last = first + 3 * BLK
    kcat[0:first] = glob_ref[0]
    vcat[0:first] = glob_ref[1]
    kcat[first:last] = kv_ref[0, win, :]
    vcat[first:last] = kv_ref[1, win, :]
    for j in range(RND):
        spot = pos[b * RND + j]
        kcat[last + j * BLK : last + (j + 1) * BLK] = rand_ref[spot, 0]
        vcat[last + j * BLK : last + (j + 1) * BLK] = rand_ref[spot, 1]

    q = q_ref[...]
    g = g_ref[...]
    count = ld_ref.shape[1]
    lse = jnp.concatenate([ld_ref[0, r : r + 1, :] for r in range(count)], axis=1) * LOG2E
    delta = jnp.concatenate([ld_ref[1, r : r + 1, :] for r in range(count)], axis=1)
    dq = None
    for pair in range((G + 3 + RND) // 2):
        span = pl.ds(pair * 2 * BLK, 2 * BLK)
        k = kcat[span, :]
        v = vcat[span, :]
        scores = dot(k, q, 1, 1) * (scaling * LOG2E)
        grads = dot(v, g, 1, 1) - delta
        halves = []
        for half in range(2):
            which = pair * 2 + half
            shift = lse
            if which >= G:
                shift = lse + bias[b * (3 + RND) + which - G]
            halves.append(jnp.exp2(scores[half * BLK : (half + 1) * BLK] - shift))
        weights = jnp.concatenate(halves, axis=0)
        score_grad = (weights * grads).astype(BF16)
        dv = dot(weights.astype(BF16), g, 1, 0)
        dk = dot(score_grad, q, 1, 0) * scaling
        part = dot(k, score_grad, 0, 0)
        dq = part if dq is None else dq + part
        for half in range(2):
            which = pair * 2 + half
            dk_half = dk[half * BLK : (half + 1) * BLK]
            dv_half = dv[half * BLK : (half + 1) * BLK]
            if which < G:
                gacc[0, which * BLK : (which + 1) * BLK, :] += dk_half
                gacc[1, which * BLK : (which + 1) * BLK, :] += dv_half
            elif which < G + 3:
                rows = pl.ds(pl.multiple_of(at + (which - G) * BLK, BLK), BLK)
                acc[0, rows, :] += dk_half
                acc[1, rows, :] += dv_half
            else:
                spot = pos[b * RND + which - G - 3]
                rpart_ref[spot, 0] = dk_half.astype(BF16)
                rpart_ref[spot, 1] = dv_half.astype(BF16)
    dq_ref[...] = (dq.T * scaling).astype(BF16)

    @pl.when(b == blocks - 1)
    def _():
        own_ref[...] = acc[:, BLK : BLK + blocks * BLK, :]
        halo_ref[0] = acc[:, 0:BLK, :].astype(BF16)
        halo_ref[1] = acc[:, BLK + blocks * BLK :, :].astype(BF16)
        gpart_ref[...] = gacc[...].astype(BF16)


def exchange_out(
    n_seq, n_head, most,
    share, dq_in, own_in, halo_in, gpart_in, rpart_in,
    dq_out, kv_out,
    halo, gall, rback, kv_sum, hs, hr, ls, ss, sr, ns, nr, gs, gr,
):
    seq, head = lax.axis_index("seq"), lax.axis_index("head")
    rows = dq_out.shape[1]
    toks = kv_out.shape[2]
    blocks = own_in.shape[1] // BLK
    greet(n_seq, n_head, seq, head)

    def rand_copy(d):
        peer = lax.rem(seq + d, n_seq)
        return remote(rpart_in.at[peer], rback.at[seq], ss.at[d], sr.at[d], seq=peer)

    def glob_copy():
        return remote(gpart_in, gall.at[seq], gs, gr.at[seq], seq=0)

    def dq_copy(d):
        peer = lax.rem(head + d, n_head)
        src = dq_in.at[pl.ds(pl.multiple_of(peer * rows, rows), rows), :]
        return remote(src, dq_out.at[head], hs.at[0, d], hr.at[0, d], head=peer)

    def kv_copy(d):
        peer = lax.rem(head + d, n_head)
        src = kv_sum.at[:, pl.ds(pl.multiple_of(peer * toks, 32), toks), :]
        return remote(src, kv_out.at[head], hs.at[1, d], hr.at[1, d], head=peer)

    up, down = lax.rem(seq + 1, n_seq), lax.rem(seq + n_seq - 1, n_seq)
    to_down = remote(halo_in.at[0], halo.at[0], ns.at[0], nr.at[0], seq=down)
    to_up = remote(halo_in.at[1], halo.at[1], ns.at[1], nr.at[1], seq=up)
    own_dq = pltpu.make_async_copy(
        dq_in.at[pl.ds(pl.multiple_of(head * rows, rows), rows), :], dq_out.at[head], ls.at[0]
    )

    to_down.start()
    to_up.start()

    @pl.when(seq > 0)
    def _():
        glob_copy().start()

    def start(d, c):
        rand_copy(d).start()
        return c

    lax.fori_loop(1, n_seq, start, 0)
    for d in range(1, n_head):
        dq_copy(d).start()
    own_dq.start()

    rback[seq] = rpart_in[seq]
    to_down.wait()
    to_up.wait()

    @pl.when(seq > 0)
    def _():
        gall[0] = jnp.zeros(gall.shape[1:], BF16)
        glob_copy().wait_send()

    @pl.when(seq == 0)
    def _():
        gall[0] = gpart_in[...]

        def arrive(d, c):
            remote(gpart_in, gall.at[d], gs, gr.at[d], seq=0).wait_recv()
            return c

        lax.fori_loop(1, n_seq, arrive, 0)

    @pl.when(seq > 0)
    def _():
        def blank(d, c):
            gall[d] = jnp.zeros(gall.shape[1:], BF16)
            return c

        lax.fori_loop(1, n_seq, blank, 0)

    def finish(d, c):
        rand_copy(d).wait()
        return c

    lax.fori_loop(1, n_seq, finish, 0)

    def gather(block, c):
        spot = pl.ds(pl.multiple_of(block * BLK, BLK), BLK)
        for part in range(2):

            def add(p, total):
                for m in range(most):
                    total = total + share[block, p * most + m] * rback[p, m, part].astype(F32)
                return total

            total = lax.fori_loop(0, n_seq, add, own_in[part, spot, :])
            kv_sum[part, spot, :] = total.astype(BF16)
        return c

    def edge(block, extra):
        spot = pl.ds(block * BLK, BLK)
        for part in range(2):

            def add(p, total):
                for m in range(most):
                    total = total + share[block, p * most + m] * rback[p, m, part].astype(F32)
                return total

            total = own_in[part, spot, :]
            for term in extra(part):
                total = total + term
            total = lax.fori_loop(0, n_seq, add, total)
            kv_sum[part, spot, :] = total.astype(BF16)

    def glob_term(part, block):
        def add(p, total):
            return total + gall[p, part, block * BLK : (block + 1) * BLK, :].astype(F32)

        return lax.fori_loop(0, n_seq, add, jnp.zeros((BLK, HD), F32))

    for block in range(blocks):
        if block < G or block == blocks - 1:

            def extra(part, block=block):
                terms = []
                if block == 0:
                    terms.append(halo[1, part].astype(F32))
                if block == blocks - 1:
                    terms.append(halo[0, part].astype(F32))
                if block < G:
                    terms.append(glob_term(part, block))
                return terms

            edge(block, extra)
    lax.fori_loop(G, blocks - 1, gather, 0)

    own_kv = pltpu.make_async_copy(
        kv_sum.at[:, pl.ds(pl.multiple_of(head * toks, 32), toks), :], kv_out.at[head], ls.at[1]
    )
    for d in range(1, n_head):
        kv_copy(d).start()
    own_kv.start()
    own_dq.wait()
    for d in range(1, n_head):
        dq_copy(d).wait()
    own_kv.wait()
    for d in range(1, n_head):
        kv_copy(d).wait()


def per_device(
    n_seq, n_head,
    queries, key_states, value_states, outputs, output_grad, logsumexp, random_owner, random_slot,
):
    toks, heads, _ = queries.shape
    group = heads // n_head
    rows = toks * group
    span = toks * n_head
    blocks = span // BLK
    per_row = blocks * RND
    most = max(1, (per_row + n_seq - 1) // n_seq)
    seq = lax.axis_index("seq")
    vmem = pl.BlockSpec(memory_space=pltpu.VMEM)
    smem = pl.BlockSpec(memory_space=pltpu.SMEM)
    hbm = pl.BlockSpec(memory_space=pl.ANY)
    dma = pltpu.SemaphoreType.DMA

    delta = jnp.sum(output_grad.astype(F32) * outputs.astype(F32), axis=-1)

    def by_head(x):
        return jnp.transpose(x.reshape(toks, n_head, group, HD), (1, 0, 2, 3)).reshape(
            n_head, rows, HD
        )

    ld = jnp.stack([logsumexp, delta]).reshape(2, toks, n_head, group)
    ld = jnp.transpose(ld, (2, 0, 1, 3)).reshape(n_head, 2, rows // 128, 128)
    kv = jnp.transpose(jnp.stack([key_states, value_states]), (2, 0, 1, 3))

    owner_table = random_owner.reshape(n_seq, per_row)
    slot_table = random_slot.reshape(n_seq, per_row)
    entry = jnp.arange(per_row, dtype=jnp.int32)
    rank_table = jnp.sum(
        (
            (owner_table[:, :, None] == owner_table[:, None, :])
            & (entry[None, :] < entry[:, None])[None]
        ).astype(jnp.int32),
        axis=2,
    )
    hits = (owner_table == seq)[:, :, None] & (
        rank_table[:, :, None] == jnp.arange(most, dtype=jnp.int32)
    )
    pick = jnp.sum(jnp.where(hits, slot_table[:, :, None] + 1, 0), axis=1).reshape(-1) - 1
    share = (pick[None, :] == jnp.arange(blocks, dtype=jnp.int32)[:, None]).astype(F32)
    my_owner = lax.dynamic_slice_in_dim(owner_table, seq, 1, 0).reshape(-1)
    my_slot = lax.dynamic_slice_in_dim(slot_table, seq, 1, 0).reshape(-1)
    my_rank = lax.dynamic_slice_in_dim(rank_table, seq, 1, 0).reshape(-1)
    pos = my_owner * most + my_rank
    ids = seq * blocks + jnp.arange(blocks, dtype=jnp.int32)
    near = ids[:, None] + jnp.arange(-1, 2, dtype=jnp.int32)[None, :]
    far = (my_owner * blocks + my_slot).reshape(blocks, RND)
    okay = jnp.concatenate(
        [
            (near >= G) & (near <= n_seq * blocks - 1),
            (far >= G) & (jnp.abs(far - ids[:, None]) >= 2),
        ],
        axis=1,
    )
    bias = jnp.where(okay, 0.0, 1e30).astype(F32).reshape(-1)

    q_loc, g_loc, ld_loc, kv_ext, glob, fetched = pl.pallas_call(
        functools.partial(exchange_in, n_seq, n_head, most),
        out_shape=[
            jax.ShapeDtypeStruct((n_head * rows, HD), BF16),
            jax.ShapeDtypeStruct((n_head * rows, HD), BF16),
            jax.ShapeDtypeStruct((n_head, 2, rows // 128, 128), F32),
            jax.ShapeDtypeStruct((2, span + 2 * BLK, HD), BF16),
            jax.ShapeDtypeStruct((2, G * BLK, HD), BF16),
            jax.ShapeDtypeStruct((n_seq, most, 2, BLK, HD), BF16),
        ],
        in_specs=[smem, hbm, hbm, vmem, vmem],
        out_specs=[vmem] * 6,
        scratch_shapes=[
            pltpu.VMEM((n_seq, most, 2, BLK, HD), BF16),
            pltpu.VMEM((blocks, 2, BLK, HD), BF16),
            dma((4, n_head)), dma((4, n_head)), dma((4,)),
            dma((n_seq,)), dma((n_seq,)), dma((2,)), dma((2,)), dma((n_seq,)), dma,
        ],
        compiler_params=pltpu.CompilerParams(
            collective_id=0, has_side_effects=True, vmem_limit_bytes=56 << 20
        ),
        name="exchange_in",
    )(jnp.maximum(pick, 0), by_head(queries), by_head(output_grad), kv, ld)

    ld_all = jnp.transpose(ld_loc, (1, 0, 2, 3)).reshape(2, n_head * rows // 128, 128)
    fetched = fetched.reshape(n_seq * most, 2, BLK, HD)
    step = BLK * group
    dq, own, halo, gpart, rpart = pl.pallas_call(
        functools.partial(attend, blocks),
        grid=(blocks,),
        out_shape=[
            jax.ShapeDtypeStruct((n_head * rows, HD), BF16),
            jax.ShapeDtypeStruct((2, span, HD), F32),
            jax.ShapeDtypeStruct((2, 2, BLK, HD), BF16),
            jax.ShapeDtypeStruct((2, G * BLK, HD), BF16),
            jax.ShapeDtypeStruct((n_seq * most, 2, BLK, HD), BF16),
        ],
        in_specs=[
            smem,
            smem,
            pl.BlockSpec((step, HD), lambda b: (b, 0)),
            pl.BlockSpec((step, HD), lambda b: (b, 0)),
            pl.BlockSpec((2, step // 128, 128), lambda b: (0, b, 0)),
            vmem, vmem, vmem,
        ],
        out_specs=[pl.BlockSpec((step, HD), lambda b: (b, 0)), vmem, vmem, vmem, vmem],
        scratch_shapes=[
            pltpu.VMEM(((G + 3 + RND) * BLK, HD), BF16),
            pltpu.VMEM(((G + 3 + RND) * BLK, HD), BF16),
            pltpu.VMEM((2, span + 2 * BLK, HD), F32),
            pltpu.VMEM((2, G * BLK, HD), F32),
        ],
        compiler_params=pltpu.CompilerParams(
            dimension_semantics=("arbitrary",), vmem_limit_bytes=56 << 20
        ),
        name="attend",
    )(pos, bias, q_loc, g_loc, ld_all, kv_ext, glob, fetched)

    dq_all, kv_all = pl.pallas_call(
        functools.partial(exchange_out, n_seq, n_head, most),
        out_shape=[
            jax.ShapeDtypeStruct((n_head, rows, HD), BF16),
            jax.ShapeDtypeStruct((n_head, 2, toks, HD), BF16),
        ],
        in_specs=[smem] + [vmem] * 5,
        out_specs=[vmem, vmem],
        scratch_shapes=[
            pltpu.VMEM((2, 2, BLK, HD), BF16),
            pltpu.VMEM((n_seq, 2, G * BLK, HD), BF16),
            pltpu.VMEM((n_seq, most, 2, BLK, HD), BF16),
            pltpu.VMEM((2, span, HD), BF16),
            dma((2, n_head)), dma((2, n_head)), dma((2,)),
            dma((n_seq,)), dma((n_seq,)), dma((2,)), dma((2,)), dma, dma((n_seq,)),
        ],
        compiler_params=pltpu.CompilerParams(
            collective_id=1, has_side_effects=True, vmem_limit_bytes=56 << 20
        ),
        name="exchange_out",
    )(share, dq, own, halo, gpart, rpart.reshape(n_seq, most, 2, BLK, HD))

    query_grad = jnp.transpose(
        dq_all.reshape(n_head, toks, group, HD), (1, 0, 2, 3)
    ).reshape(toks, heads, HD)
    key_grad = jnp.transpose(kv_all[:, 0], (1, 0, 2))
    value_grad = jnp.transpose(kv_all[:, 1], (1, 0, 2))
    return query_grad, key_grad, value_grad


def solution(mesh):
    wide = P(("seq", "head"), None, None)
    return jax.shard_map(
        functools.partial(per_device, mesh.shape["seq"], mesh.shape["head"]),
        mesh=mesh,
        in_specs=(wide, wide, wide, wide, wide, P(("seq", "head"), None), P(), P()),
        out_specs=(wide, wide, wide),
        check_vma=False,
    )
```

time: 562 us -> 202 us (0.36)
  the two profiles are of different devices: /device:TPU:0 before, /device:TPU:11 now
where the time goes in v1:
time: 202 us
  Pallas kernels  178 us (88%)
  local copies, waits for them, and re-layouts  16.8 us (8%)
  other arithmetic  5.77 us (3%)
    pallas_call x1, Pallas kernels, per_device(): pl.pallas_call(functools.partial(exchange_out, n_seq, n_head, most), out_...  80.2 us
    pallas_call x1, Pallas kernels, per_device(): pl.pallas_call(functools.partial(exchange_in, n_seq, n_head, most), out_s...  67.1 us
    pallas_call x1, Pallas kernels, per_device(): pl.pallas_call(functools.partial(attend, blocks), grid=(blocks,), out_sha...  31.1 us

profile of v1, /device:TPU:11, one launch (start us, length us, event | category | flops | bytes accessed | tf_op | source)
XLA Modules:
  0.0 201.7 jit_solution(7624349477068681481)
XLA Ops:
  0.6 0.9 copy.66
  1.7 0.1 copy.81
  1.8 0.8 copy.63
  2.7 0.6 convert_reduce_fusion
  3.3 0.8 add_reduce_fusion
  4.4 0.6 select_n.20.bias
  5.0 0.1 select_reduce_fusion
  5.4 0.5 broadcast_maximum_fusion.pick
  5.9 1.3 copy_bitcast_fusion.3
  7.2 0.9 maximum_bitcast_fusion.kv_in
  8.1 3.2 %copy_bitcast_fusion.1 = (bf16[4,2304,128]{2,1,0:T(8,128)(2,1)}, bf16[4,2304,128]{2,1,0:T(8,128)(2,1)}) fusion(bf16[288,32,128]{2,1,0:T(8,128)(2,1)S(1)} %copy-done, bf16[288,32,128]{2,1,0:T(8,128)(2,1)S(1)} %copy-done.1), kind=kLoop, calls=%fused_computation.2 | loop fusion | bytes 9437184 | tf_op jit(solution)/shard_map/reshape | solution.py:419
  11.3 1.3 multiply_reduce_fusion
  12.7 0.7 maximum_bitcast_fusion.1
  13.4 1.3 copy.75
  14.7 1.2 reshape.110.ld_in
  15.8 67.1 %exchange_in.1 = (bf16[9216,128]{1,0:T(8,128)(2,1)}, bf16[9216,128]{1,0:T(8,128)(2,1)}, f32[4,2,18,128]{3,2,1,0:T(8,128)}, bf16[2,1408,128]{2,1,0:T(8,128)(2,1)}...) custom-call(s32[32]{0:T(128)} %broadcast_maximum_fusion.pick, ...), custom_call_target="tpu_custom_call" | custom-call | tf_op jit(solution)/shard_map/exchange_in/pallas_call | solution.py:458
  82.9 0.9 copy.76
  83.9 0.6 copy.77.ld_ref
  84.5 31.1 %attend.1 = (bf16[9216,128]{1,0:T(8,128)(2,1)}, f32[2,1152,128]{2,1,0:T(8,128)}, bf16[2,2,128,128]{3,2,1,0:T(8,128)(2,1)}, bf16[2,256,128]{2,1,0:T(8,128)(2,1)}, bf16[32,2,128,128]{3,2,1,0:T(8,128)(2,1)}) custom-call(s32[27]{0:T(128)} %get-tuple-element.45.pos, f32[54]{0:T(128)} %select_n.20.bias, bf16[9216,128]{1,0:T(8,128)(2,1)} %get-tuple-element.16.q_ref, ...), custom_call_target="tpu_custom_call" | custom-call | tf_op jit(solution)/shard_map/attend/pallas_call | solution.py:485
  115.6 0.6 fusion.1.share
  116.2 80.2 %exchange_out.1 = (bf16[4,2304,128]{2,1,0:T(8,128)(2,1)}, bf16[4,2,288,128]{3,2,1,0:T(8,128)(2,1)}) custom-call(f32[9,32]{1,0:T(8,128)} %fusion.1.share, bf16[9216,128]{1,0:T(8,128)(2,1)} %get-tuple-element.22.dq_in, f32[2,1152,128]{2,1,0:T(8,128)} %get-tuple-element.23.own_in, bf16[2,2,128,128]{3,2,1,0:T(8,128)(2,1)} %get-tuple-element.24.halo_in, ...), custom_call_target="tpu_custom_call" | custom-call | tf_op jit(solution)/shard_map/exchange_out/pallas_call | solution.py:516
  196.4 3.5 %copy_bitcast_fusion = bf16[288,32,128]{2,1,0:T(8,128)(2,1)} fusion(bf16[4,2304,128]{2,1,0:T(8,128)(2,1)} %get-tuple-element.27), kind=kLoop, calls=%fused_computation.1 | loop fusion | bytes 4718592 | tf_op jit(solution)/shard_map/reshape | solution.py:540
  200.0 0.9 copy.79
  200.9 0.9 copy.80
  (28 shorter events, 0.9 us)
Async XLA Ops:
  0.6 7.5 %copy-start = (bf16[288,32,128]{2,1,0:T(8,128)(2,1)S(1)}, bf16[288,32,128]{2,1,0:T(8,128)(2,1)}, u32[]{:S(2)}) copy-start(bf16[288,32,128]{2,1,0:T(8,128)(2,1)} %param.8) | copy-start | bytes 7077892
  5.4 2.8 %copy-start.1 = (bf16[288,32,128]{2,1,0:T(8,128)(2,1)S(1)}, bf16[288,32,128]{2,1,0:T(8,128)(2,1)}, u32[]{:S(2)}) copy-start(bf16[288,32,128]{2,1,0:T(8,128)(2,1)} %param.12) | copy-start | bytes 7077892
  8.1 3.2 %copy-start.2 = (bf16[288,32,128]{2,1,0:T(8,128)(2,1)S(1)}, bf16[288,32,128]{2,1,0:T(8,128)(2,1)}, u32[]{:S(2)}) copy-start(bf16[288,32,128]{2,1,0:T(8,128)(2,1)} %param.11) | copy-start | bytes 7077892
  11.3 1.4 copy-start.4
  196.4 3.5 %copy-start.3 = (bf16[4,2,288,128]{3,2,1,0:T(8,128)(2,1)S(1)}, bf16[4,2,288,128]{3,2,1,0:T(8,128)(2,1)}, u32[]{:S(2)}) copy-start(bf16[4,2,288,128]{3,2,1,0:T(8,128)(2,1)} %get-tuple-element.28) | copy-start | bytes 1769476

commit v2 on v1

v2 whole, which is shorter than its diff:
```python
import functools
import math

import jax
import jax.numpy as jnp
from jax import lax
from jax.experimental import pallas as pl
from jax.experimental.pallas import tpu as pltpu
from jax.sharding import PartitionSpec as P

HD = 128
BLK = 128
G = 2
RND = 3
MESH = pl.DeviceIdType.MESH
F32 = jnp.float32
BF16 = jnp.bfloat16
LOG2E = math.log2(math.e)


def greet(n_seq, n_head, seq, head):
    barrier = pltpu.get_barrier_semaphore()

    def to_head(d, c):
        pl.semaphore_signal(
            barrier, inc=1, device_id={"head": lax.rem(head + d, n_head)}, device_id_type=MESH
        )
        return c

    def to_seq(d, c):
        pl.semaphore_signal(
            barrier, inc=1, device_id={"seq": lax.rem(seq + d, n_seq)}, device_id_type=MESH
        )
        return c

    lax.fori_loop(1, n_head, to_head, 0)
    lax.fori_loop(1, n_seq, to_seq, 0)
    pl.semaphore_wait(barrier, n_head + n_seq - 2)


def remote(src, dst, send, recv, **where):
    return pltpu.make_async_remote_copy(
        src_ref=src,
        dst_ref=dst,
        send_sem=send,
        recv_sem=recv,
        device_id=where,
        device_id_type=MESH,
    )


def dot(a, b, ca, cb):
    return lax.dot_general(a, b, (((ca,), (cb,)), ((), ())), preferred_element_type=F32)


def pair_grads(k, v, shifts, q, g, delta, scaling):
    scores = dot(k, q, 1, 1) * (scaling * LOG2E)
    weights = jnp.concatenate(
        [jnp.exp2(scores[i * BLK : (i + 1) * BLK] - shift) for i, shift in enumerate(shifts)],
        axis=0,
    )
    score_grad = (weights * (dot(v, g, 1, 1) - delta)).astype(BF16)
    dv = dot(weights.astype(BF16), g, 1, 0)
    dk = dot(score_grad, q, 1, 0) * scaling
    return dk, dv, dot(k, score_grad, 0, 0)


def fused(
    n_seq, n_head, most, blocks,
    pick, pos, back, bias, share, q_in, g_in, kv_in, ld_in,
    dq_out, kv_out,
    q_all, g_all, ld_all, kv_ext, glob, rand, picked, held, acc, gacc, dq_acc, dq_all,
    rpart, rback, halo_part, halo, gpart, gall, kv_sum,
    hs, hr, ls, ss, sr, ns, nr, gs, gr, rs, rr,
):
    seq, head = lax.axis_index("seq"), lax.axis_index("head")
    rows = q_in.shape[1]
    toks = kv_in.shape[2]
    span = n_head * toks
    lines = rows // 128
    step = rows * n_head // blocks
    scaling = 1.0 / HD**0.5
    greet(n_seq, n_head, seq, head)

    def partner(d):
        base = lax.rem(head + 2 * (d // 2), n_head)
        return base + (1 - 2 * lax.rem(base, 2)) if d % 2 else base

    mine = pl.ds(pl.multiple_of(head * rows, rows), rows)
    q_to = q_all.at[mine, :]
    g_to = g_all.at[mine, :]
    kv_to = kv_ext.at[:, pl.ds(pl.multiple_of(BLK + head * toks, 32), toks), :]
    ld_to = ld_all.at[:, pl.ds(head * lines, lines)]

    def head_copy(kind, d):
        peer = partner(d)
        src, dst = (
            (kv_in.at[peer], kv_to),
            (ld_in.at[peer], ld_to),
            (q_in.at[peer], q_to),
            (g_in.at[peer], g_to),
        )[kind]
        return remote(src, dst, hs.at[kind, d], hr.at[kind, d], head=peer)

    own = [
        pltpu.make_async_copy(kv_in.at[head], kv_to, ls.at[0]),
        pltpu.make_async_copy(ld_in.at[head], ld_to, ls.at[1]),
        pltpu.make_async_copy(q_in.at[head], q_to, ls.at[2]),
        pltpu.make_async_copy(g_in.at[head], g_to, ls.at[3]),
    ]
    for kind in range(4):
        own[kind].start()
    for kind in range(4):
        for d in list(range(2, n_head)) + [1]:
            head_copy(kind, d).start()
    own[0].wait()
    for d in range(1, n_head):
        head_copy(0, d).wait_recv()

    up, down = lax.rem(seq + 1, n_seq), lax.rem(seq + n_seq - 1, n_seq)
    to_up = remote(
        kv_ext.at[:, pl.ds(span, BLK), :], kv_ext.at[:, pl.ds(0, BLK), :],
        ns.at[0], nr.at[0], seq=up,
    )
    to_down = remote(
        kv_ext.at[:, pl.ds(BLK, BLK), :], kv_ext.at[:, pl.ds(BLK + span, BLK), :],
        ns.at[1], nr.at[1], seq=down,
    )

    def rand_copy(d):
        peer = lax.rem(seq + d, n_seq)
        return remote(
            picked.at[pl.ds(peer * most, most)], rand.at[pl.ds(seq * most, most)],
            ss.at[d], sr.at[d], seq=peer,
        )

    def glob_copy(d):
        return remote(kv_ext.at[:, pl.ds(BLK, G * BLK), :], glob, gs.at[d], gr.at[0], seq=d)

    def loop(low, high, body):
        def run(i, c):
            body(i)
            return c

        lax.fori_loop(low, high, run, 0)

    def fill(i):
        picked[i] = held[pick[i]]

    for block in range(blocks):
        held[block] = kv_ext[:, (block + 1) * BLK : (block + 2) * BLK, :]
    loop(0, n_seq * most, fill)
    to_up.start()
    to_down.start()

    @pl.when(seq == 0)
    def _():
        loop(1, n_seq, lambda d: glob_copy(d).start())
        glob[...] = kv_ext[:, BLK : BLK + G * BLK, :]

    loop(1, n_seq, lambda d: rand_copy(d).start())
    rand[pl.ds(seq * most, most)] = picked[pl.ds(seq * most, most)]

    acc[...] = jnp.zeros_like(acc)
    gacc[...] = jnp.zeros_like(gacc)
    to_up.wait()
    to_down.wait()

    @pl.when(seq > 0)
    def _():
        glob_copy(0).wait_recv()

    for kind in range(1, 4):
        own[kind].wait()
        head_copy(kind, 1).wait_recv()
    for d in range(2, n_head):
        head_copy(1, d).wait_recv()

    turn = head // (n_head // 2)

    def order(i):
        return i + turn * (blocks - 1 - 2 * i)

    def operands(b):
        spot = pl.ds(pl.multiple_of(b * step, step), step)
        per = step // 128

        def lanes(part):
            tile = ld_all[part, pl.ds(b * per, per)]
            return jnp.concatenate([tile[r] for r in range(per)], axis=1)

        return q_all[spot, :], g_all[spot, :], lanes(0) * LOG2E, lanes(1)

    def near(i, fresh):
        b = order(i)
        q, g, lse, delta = operands(b)
        at = pl.multiple_of(b * BLK, BLK)
        win = pl.ds(at, 3 * BLK)
        dk, dv, dq = pair_grads(glob[0], glob[1], [lse] * G, q, g, delta, scaling)
        gacc[0] += dk
        gacc[1] += dv
        shifts = [lse + bias[b * (3 + RND) + j] for j in range(3)]
        dk, dv, more = pair_grads(kv_ext[0, win, :], kv_ext[1, win, :], shifts, q, g, delta, scaling)
        acc[0, win, :] += dk
        acc[1, win, :] += dv
        if fresh:
            dq_acc[b] = dq + more
        else:
            total = dq_acc[b] + dq + more
            dq_all[pl.ds(pl.multiple_of(b * step, step), step), :] = (total.T * scaling).astype(BF16)

    def far(i, fresh):
        b = order(i)
        q, g, lse, delta = operands(b)
        found = [rand[pos[b * RND + j]] for j in range(RND)]
        k = jnp.concatenate([f[0] for f in found], axis=0)
        v = jnp.concatenate([f[1] for f in found], axis=0)
        shifts = [lse + bias[b * (3 + RND) + 3 + j] for j in range(RND)]
        dk, dv, dq = pair_grads(k, v, shifts, q, g, delta, scaling)
        for j in range(RND):
            rpart[b * RND + j, 0] = dk[j * BLK : (j + 1) * BLK].astype(BF16)
            rpart[b * RND + j, 1] = dv[j * BLK : (j + 1) * BLK].astype(BF16)
        if fresh:
            dq_acc[b] = dq
        else:
            total = dq_acc[b] + dq
            dq_all[pl.ds(pl.multiple_of(b * step, step), step), :] = (total.T * scaling).astype(BF16)

    early = span // 2 // BLK
    loop(0, early, lambda i: near(i, True))
    loop(1, n_seq, lambda d: rand_copy(d).wait())
    loop(0, early, lambda i: far(i, False))
    for kind in range(2, 4):
        for d in range(2, n_head):
            head_copy(kind, d).wait_recv()
    loop(early, blocks, lambda i: far(i, True))

    def gather(i):
        picked[i] = rpart[back[i]]

    def back_copy(d):
        peer = lax.rem(seq + d, n_seq)
        return remote(
            picked.at[pl.ds(peer * most, most)], rback.at[pl.ds(seq * most, most)],
            rs.at[d], rr.at[d], seq=peer,
        )

    loop(0, n_seq * most, gather)
    rback[pl.ds(seq * most, most)] = picked[pl.ds(seq * most, most)]
    loop(1, n_seq, lambda d: back_copy(d).start())
    loop(early, blocks, lambda i: near(i, False))

    halo_part[0] = acc[:, 0:BLK, :].astype(BF16)
    halo_part[1] = acc[:, BLK + span :, :].astype(BF16)
    gpart[...] = gacc[...].astype(BF16)

    def dq_copy(d):
        peer = partner(d)
        src = dq_all.at[pl.ds(pl.multiple_of(peer * rows, rows), rows), :]
        return remote(src, dq_out.at[head], hs.at[4, d], hr.at[4, d], head=peer)

    def kv_copy(d):
        peer = partner(d)
        src = kv_sum.at[:, pl.ds(pl.multiple_of(peer * toks, 32), toks), :]
        return remote(src, kv_out.at[head], hs.at[5, d], hr.at[5, d], head=peer)

    def part_copy():
        return remote(gpart, gall.at[seq], gs.at[0], gr.at[seq], seq=0)

    down_grad = remote(halo_part.at[0], halo.at[0], ns.at[2], nr.at[2], seq=down)
    up_grad = remote(halo_part.at[1], halo.at[1], ns.at[3], nr.at[3], seq=up)
    own_dq = pltpu.make_async_copy(dq_all.at[mine, :], dq_out.at[head], ls.at[4])
    for d in list(range(2, n_head)) + [1]:
        dq_copy(d).start()
    own_dq.start()
    down_grad.start()
    up_grad.start()

    @pl.when(seq > 0)
    def _():
        part_copy().start()

    for kind in range(4):
        for d in range(1, n_head):
            head_copy(kind, d).wait_send()

    @pl.when(seq == 0)
    def _():
        loop(1, n_seq, lambda d: glob_copy(d).wait_send())
        gall[0] = gpart[...]

        def arrive(d):
            remote(gpart, gall.at[d], gs.at[0], gr.at[d], seq=0).wait_recv()

        loop(1, n_seq, arrive)

        def add(d):
            gacc[...] += gall[d].astype(F32)

        loop(1, n_seq, add)
        acc[:, BLK : BLK + G * BLK, :] += gacc[...]

    @pl.when(seq > 0)
    def _():
        part_copy().wait_send()

    down_grad.wait()
    up_grad.wait()
    acc[:, BLK : 2 * BLK, :] += halo[1].astype(F32)
    acc[:, span : span + BLK, :] += halo[0].astype(F32)
    loop(1, n_seq, lambda d: back_copy(d).wait())

    def total(block):
        spot = pl.ds(pl.multiple_of(block * BLK, BLK), BLK)
        over = pl.ds(pl.multiple_of(block * BLK + BLK, BLK), BLK)
        for part in range(2):

            def add(i, value):
                return value + share[block, i] * rback[i, part].astype(F32)

            value = lax.fori_loop(0, n_seq * most, add, acc[part, over, :])
            kv_sum[part, spot, :] = value.astype(BF16)

    loop(0, blocks, total)
    own_kv = pltpu.make_async_copy(
        kv_sum.at[:, pl.ds(pl.multiple_of(head * toks, 32), toks), :], kv_out.at[head], ls.at[5]
    )
    for d in list(range(2, n_head)) + [1]:
        kv_copy(d).start()
    own_kv.start()
    own_dq.wait()
    for d in range(1, n_head):
        dq_copy(d).wait()
    own_kv.wait()
    for d in range(1, n_head):
        kv_copy(d).wait()


def per_device(
    n_seq, n_head,
    queries, key_states, value_states, outputs, output_grad, logsumexp, random_owner, random_slot,
):
    toks, heads, _ = queries.shape
    group = heads // n_head
    rows = toks * group
    span = toks * n_head
    blocks = span // BLK
    per_row = blocks * RND
    most = max(1, (per_row + n_seq - 1) // n_seq)
    seq = lax.axis_index("seq")
    vmem = pl.BlockSpec(memory_space=pltpu.VMEM)
    smem = pl.BlockSpec(memory_space=pltpu.SMEM)
    hbm = pl.BlockSpec(memory_space=pl.ANY)
    dma = pltpu.SemaphoreType.DMA

    delta = jnp.sum(output_grad.astype(F32) * outputs.astype(F32), axis=-1)

    def by_head(x):
        return jnp.transpose(x.reshape(toks, n_head, group, HD), (1, 0, 2, 3)).reshape(
            n_head, rows, HD
        )

    ld = jnp.stack([logsumexp, delta]).reshape(2, toks, n_head, group)
    ld = jnp.transpose(ld, (2, 0, 1, 3)).reshape(n_head, 2, rows // 128, 1, 128)
    kv = jnp.transpose(jnp.stack([key_states, value_states]), (2, 0, 1, 3))

    owner_table = random_owner.reshape(n_seq, per_row)
    slot_table = random_slot.reshape(n_seq, per_row)
    entry = jnp.arange(per_row, dtype=jnp.int32)
    rank_table = jnp.sum(
        (
            (owner_table[:, :, None] == owner_table[:, None, :])
            & (entry[None, :] < entry[:, None])[None]
        ).astype(jnp.int32),
        axis=2,
    )
    hits = (owner_table == seq)[:, :, None] & (
        rank_table[:, :, None] == jnp.arange(most, dtype=jnp.int32)
    )
    pick = jnp.sum(jnp.where(hits, slot_table[:, :, None] + 1, 0), axis=1).reshape(-1) - 1
    share = (pick[None, :] == jnp.arange(blocks, dtype=jnp.int32)[:, None]).astype(F32)
    my_owner = lax.dynamic_slice_in_dim(owner_table, seq, 1, 0).reshape(-1)
    my_slot = lax.dynamic_slice_in_dim(slot_table, seq, 1, 0).reshape(-1)
    my_rank = lax.dynamic_slice_in_dim(rank_table, seq, 1, 0).reshape(-1)
    pos = my_owner * most + my_rank
    ids = seq * blocks + jnp.arange(blocks, dtype=jnp.int32)
    near = ids[:, None] + jnp.arange(-1, 2, dtype=jnp.int32)[None, :]
    far = (my_owner * blocks + my_slot).reshape(blocks, RND)
    okay = jnp.concatenate(
        [
            (near >= G) & (near <= n_seq * blocks - 1),
            (far >= G) & (jnp.abs(far - ids[:, None]) >= 2),
        ],
        axis=1,
    )
    bias = jnp.where(okay, 0.0, 1e30).astype(F32).reshape(-1)

    back = jnp.sum(
        jnp.where(
            pos[None, :] == jnp.arange(n_seq * most, dtype=jnp.int32)[:, None],
            jnp.arange(per_row, dtype=jnp.int32)[None, :],
            0,
        ),
        axis=1,
    )
    slots = n_seq * most
    step = BLK * group
    dq_all, kv_all = pl.pallas_call(
        functools.partial(fused, n_seq, n_head, most, blocks),
        out_shape=[
            jax.ShapeDtypeStruct((n_head, rows, HD), BF16),
            jax.ShapeDtypeStruct((n_head, 2, toks, HD), BF16),
        ],
        in_specs=[smem] * 5 + [hbm, hbm, vmem, vmem],
        out_specs=[vmem, vmem],
        scratch_shapes=[
            pltpu.VMEM((n_head * rows, HD), BF16),
            pltpu.VMEM((n_head * rows, HD), BF16),
            pltpu.VMEM((2, n_head * rows // 128, 1, 128), F32),
            pltpu.VMEM((2, span + 2 * BLK, HD), BF16),
            pltpu.VMEM((2, G * BLK, HD), BF16),
            pltpu.VMEM((slots, 2, BLK, HD), BF16),
            pltpu.VMEM((slots, 2, BLK, HD), BF16),
            pltpu.VMEM((blocks, 2, BLK, HD), BF16),
            pltpu.VMEM((2, span + 2 * BLK, HD), F32),
            pltpu.VMEM((2, G * BLK, HD), F32),
            pltpu.VMEM((blocks, HD, step), F32),
            pltpu.VMEM((n_head * rows, HD), BF16),
            pltpu.VMEM((per_row, 2, BLK, HD), BF16),
            pltpu.VMEM((slots, 2, BLK, HD), BF16),
            pltpu.VMEM((2, 2, BLK, HD), BF16),
            pltpu.VMEM((2, 2, BLK, HD), BF16),
            pltpu.VMEM((2, G * BLK, HD), BF16),
            pltpu.VMEM((n_seq, 2, G * BLK, HD), BF16),
            pltpu.VMEM((2, span, HD), BF16),
            dma((6, n_head)), dma((6, n_head)), dma((6,)),
            dma((n_seq,)), dma((n_seq,)), dma((4,)), dma((4,)), dma((n_seq,)), dma((n_seq,)),
            dma((n_seq,)), dma((n_seq,)),
        ],
        compiler_params=pltpu.CompilerParams(
            collective_id=0, has_side_effects=True, vmem_limit_bytes=60 << 20
        ),
        name="fused",
    )(jnp.maximum(pick, 0), pos, back, bias, share, by_head(queries), by_head(output_grad), kv, ld)

    query_grad = jnp.transpose(
        dq_all.reshape(n_head, toks, group, HD), (1, 0, 2, 3)
    ).reshape(toks, heads, HD)
    key_grad = jnp.transpose(kv_all[:, 0], (1, 0, 2))
    value_grad = jnp.transpose(kv_all[:, 1], (1, 0, 2))
    return query_grad, key_grad, value_grad


def solution(mesh):
    wide = P(("seq", "head"), None, None)
    return jax.shard_map(
        functools.partial(per_device, mesh.shape["seq"], mesh.shape["head"]),
        mesh=mesh,
        in_specs=(wide, wide, wide, wide, wide, P(("seq", "head"), None), P(), P()),
        out_specs=(wide, wide, wide),
        check_vma=False,
    )
```

time: 202 us -> 171 us (0.85)
  the two profiles are of different devices: /device:TPU:11 before, /device:TPU:0 now
where the time goes in v2:
time: 171 us; the launch traced here: 169 us
  Pallas kernels  145 us (85%)
  local copies, waits for them, and re-layouts  15.7 us (9%)
  other arithmetic  8.27 us (5%)
    pallas_call x1, Pallas kernels, per_device(): pl.pallas_call(functools.partial(fused, n_seq, n_head, most, blocks), out...  145 us
    reshape x1, local copies, waits for them, and re-layouts, by_head(): jnp.transpose(x.reshape(toks, n_head, group, HD), (1, 0, 2, 3))  4.76 us
    reduce_sum x1, other arithmetic, per_device(): delta = jnp.sum(output_grad.astype(F32) * outputs.astype(F32), axis=-1)  3.73 us
    unnamed x17, local copies, waits for them, and re-layouts  3.56 us
    reshape x1, local copies, waits for them, and re-layouts, per_device(): query_grad = jnp.transpose(dq_all.reshape(n_head, toks, group, HD), (1, 0...  3.54 us

profile of v2, /device:TPU:0, one launch (start us, length us, event | category | flops | bytes accessed | tf_op | source)
XLA Modules:
  0.0 169.3 jit_solution(15942575801763971063)
XLA Ops:
  0.7 0.9 copy.59
  1.7 0.1 copy.60
  1.8 0.6 convert_reduce_fusion
  2.5 0.8 copy.62
  3.4 0.1 select_reduce_fusion.1
  3.5 0.1 copy.63
  3.6 0.1 sub.13
  3.7 0.6 broadcast_maximum_fusion.pick
  4.3 0.6 fusion.2.share
  4.9 0.1 copy.76
  5.0 0.2 add_reduce_fusion
  5.2 0.6 select_reduce_fusion.back
  6.1 0.6 select_n.25.bias
  6.7 3.7 %multiply_reduce_fusion = f32[288,32]{1,0:T(8,128)S(1)} fusion(bf16[288,32,128]{2,1,0:T(8,128)(2,1)} %param.11, bf16[288,32,128]{2,1,0:T(8,128)(2,1)} %param.12), kind=kLoop, calls=%fused_computation | loop fusion | flops 4709376 | bytes 4755456 | tf_op jit(solution)/shard_map/reduce_sum | solution.py:356
  10.4 0.1 copy.70
  10.5 0.7 maximum_bitcast_fusion.1
  11.3 0.9 maximum_bitcast_fusion.kv_in
  12.2 1.3 copy.71
  13.4 1.2 reshape.104.ld_in
  14.7 4.8 %copy_bitcast_fusion.1 = (bf16[4,2304,128]{2,1,0:T(8,128)(2,1)}, bf16[4,2304,128]{2,1,0:T(8,128)(2,1)}) fusion(bf16[288,32,128]{2,1,0:T(8,128)(2,1)S(1)} %copy-done, bf16[288,32,128]{2,1,0:T(8,128)(2,1)} %param.12), kind=kLoop, calls=%fused_computation.2 | loop fusion | bytes 9437184 | tf_op jit(solution)/shard_map/reshape | solution.py:359
  19.4 144.5 %fused.1 = (bf16[4,2304,128]{2,1,0:T(8,128)(2,1)}, bf16[4,2,288,128]{3,2,1,0:T(8,128)(2,1)}) custom-call(s32[32]{0:T(128)} %broadcast_maximum_fusion.pick, s32[27]{0:T(128)} %copy-done.5, s32[32]{0:T(128)} %select_reduce_fusion.back, f32[54]{0:T(128)} %select_n.25.bias, f32[9,32]{1,0:T(8,128)} %fusion.2.share, bf16[4,2304,128]{2,1,0:T(8,128)(2,1)} %get-tuple-element.31.q_in, ...), custom_call_target="tpu_custom_call" | custom-call | tf_op jit(solution)/shard_map/fused/pallas_call | solution.py:408
  164.0 3.5 %copy_bitcast_fusion = bf16[288,32,128]{2,1,0:T(8,128)(2,1)} fusion(bf16[4,2304,128]{2,1,0:T(8,128)(2,1)} %get-tuple-element.5), kind=kLoop, calls=%fused_computation.1 | loop fusion | bytes 4718592 | tf_op jit(solution)/shard_map/reshape | solution.py:448
  167.6 0.9 copy.75
  168.4 0.9 copy.74
  (27 shorter events, 0.7 us)
Async XLA Ops:
  0.6 14.0 %copy-start = (bf16[288,32,128]{2,1,0:T(8,128)(2,1)S(1)}, bf16[288,32,128]{2,1,0:T(8,128)(2,1)}, u32[]{:S(2)}) copy-start(bf16[288,32,128]{2,1,0:T(8,128)(2,1)} %param.8) | copy-start | bytes 7077892
  5.2 5.3 %copy-start.5 = (s32[27]{0:T(128)}, s32[27]{0:T(128)S(1)}, u32[]{:S(2)}) copy-start(s32[27]{0:T(128)S(1)} %get-tuple-element.23.pos) | copy-start | bytes 328
  6.7 3.9 %copy-start.4 = (f32[288,32]{0,1:T(8,128)S(1)}, f32[288,32]{0,1:T(8,128)}, u32[]{:S(2)}) copy-start(f32[288,32]{0,1:T(8,128)} %param.13) | copy-start | bytes 110596
  6.7 4.5 %copy-start.2 = (bf16[288,4,128]{2,1,0:T(4,128)(2,1)S(1)}, bf16[288,4,128]{2,1,0:T(4,128)(2,1)}, u32[]{:S(2)}) copy-start(bf16[288,4,128]{2,1,0:T(4,128)(2,1)} %param.10) | copy-start | bytes 884740
  6.7 4.5 %copy-start.3 = (bf16[288,4,128]{2,1,0:T(4,128)(2,1)S(1)}, bf16[288,4,128]{2,1,0:T(4,128)(2,1)}, u32[]{:S(2)}) copy-start(bf16[288,4,128]{2,1,0:T(4,128)(2,1)} %param.9) | copy-start | bytes 884740
  164.0 3.5 %copy-start.1 = (bf16[4,2,288,128]{3,2,1,0:T(8,128)(2,1)S(1)}, bf16[4,2,288,128]{3,2,1,0:T(8,128)(2,1)}, u32[]{:S(2)}) copy-start(bf16[4,2,288,128]{3,2,1,0:T(8,128)(2,1)} %get-tuple-element.6) | copy-start | bytes 1769476

commit v3 on v2

--- a/solution.py
+++ b/solution.py
@@ -74,8 +74,9 @@
     hs, hr, ls, ss, sr, ns, nr, gs, gr, rs, rr,
 ):
     seq, head = lax.axis_index("seq"), lax.axis_index("head")
-    rows = q_in.shape[1]
     toks = kv_in.shape[2]
+    group = q_in.shape[1] // n_head
+    rows = toks * group
     span = n_head * toks
     lines = rows // 128
     step = rows * n_head // blocks
@@ -87,26 +88,30 @@
         return base + (1 - 2 * lax.rem(base, 2)) if d % 2 else base
 
     mine = pl.ds(pl.multiple_of(head * rows, rows), rows)
-    q_to = q_all.at[mine, :]
-    g_to = g_all.at[mine, :]
+    here = pl.ds(pl.multiple_of(head * toks, toks), toks)
+    q_to = q_all.at[here]
+    g_to = g_all.at[here]
     kv_to = kv_ext.at[:, pl.ds(pl.multiple_of(BLK + head * toks, 32), toks), :]
     ld_to = ld_all.at[:, pl.ds(head * lines, lines)]
+
+    def heads_of(ref, peer):
+        return ref.at[:, pl.ds(pl.multiple_of(peer * group, group), group), :]
 
     def head_copy(kind, d):
         peer = partner(d)
         src, dst = (
             (kv_in.at[peer], kv_to),
             (ld_in.at[peer], ld_to),
-            (q_in.at[peer], q_to),
-            (g_in.at[peer], g_to),
+            (heads_of(q_in, peer), q_to),
+            (heads_of(g_in, peer), g_to),
         )[kind]
         return remote(src, dst, hs.at[kind, d], hr.at[kind, d], head=peer)
 
     own = [
         pltpu.make_async_copy(kv_in.at[head], kv_to, ls.at[0]),
         pltpu.make_async_copy(ld_in.at[head], ld_to, ls.at[1]),
-        pltpu.make_async_copy(q_in.at[head], q_to, ls.at[2]),
-        pltpu.make_async_copy(g_in.at[head], g_to, ls.at[3]),
+        pltpu.make_async_copy(heads_of(q_in, head), q_to, ls.at[2]),
+        pltpu.make_async_copy(heads_of(g_in, head), g_to, ls.at[3]),
     ]
     for kind in range(4):
         own[kind].start()
@@ -182,14 +187,15 @@
         return i + turn * (blocks - 1 - 2 * i)
 
     def operands(b):
-        spot = pl.ds(pl.multiple_of(b * step, step), step)
+        spot = pl.ds(pl.multiple_of(b * BLK, BLK), BLK)
         per = step // 128
 
         def lanes(part):
             tile = ld_all[part, pl.ds(b * per, per)]
             return jnp.concatenate([tile[r] for r in range(per)], axis=1)
 
-        return q_all[spot, :], g_all[spot, :], lanes(0) * LOG2E, lanes(1)
+        flat = (step, HD)
+        return q_all[spot].reshape(flat), g_all[spot].reshape(flat), lanes(0) * LOG2E, lanes(1)
 
     def near(i, fresh):
         b = order(i)
@@ -308,20 +314,26 @@
     up_grad.wait()
     acc[:, BLK : 2 * BLK, :] += halo[1].astype(F32)
     acc[:, span : span + BLK, :] += halo[0].astype(F32)
-    loop(1, n_seq, lambda d: back_copy(d).wait())
-
-    def total(block):
-        spot = pl.ds(pl.multiple_of(block * BLK, BLK), BLK)
-        over = pl.ds(pl.multiple_of(block * BLK + BLK, BLK), BLK)
-        for part in range(2):
-
-            def add(i, value):
-                return value + share[block, i] * rback[i, part].astype(F32)
-
-            value = lax.fori_loop(0, n_seq * most, add, acc[part, over, :])
-            kv_sum[part, spot, :] = value.astype(BF16)
-
-    loop(0, blocks, total)
+    def absorb(d):
+        base = lax.rem(seq + n_seq - d, n_seq) * most
+
+        def block_sum(block):
+            over = pl.ds(pl.multiple_of(block * BLK + BLK, BLK), BLK)
+            for part in range(2):
+                value = acc[part, over, :]
+                for m in range(most):
+                    value = value + share[block, base + m] * rback[base + m, part].astype(F32)
+                acc[part, over, :] = value
+
+        loop(0, blocks, block_sum)
+
+    def take(d):
+        back_copy(d).wait()
+        absorb(d)
+
+    absorb(0)
+    loop(1, n_seq, take)
+    kv_sum[...] = acc[:, BLK : BLK + span, :].astype(BF16)
     own_kv = pltpu.make_async_copy(
         kv_sum.at[:, pl.ds(pl.multiple_of(head * toks, 32), toks), :], kv_out.at[head], ls.at[5]
     )
@@ -355,11 +367,6 @@
 
     delta = jnp.sum(output_grad.astype(F32) * outputs.astype(F32), axis=-1)
 
-    def by_head(x):
-        return jnp.transpose(x.reshape(toks, n_head, group, HD), (1, 0, 2, 3)).reshape(
-            n_head, rows, HD
-        )
-
     ld = jnp.stack([logsumexp, delta]).reshape(2, toks, n_head, group)
     ld = jnp.transpose(ld, (2, 0, 1, 3)).reshape(n_head, 2, rows // 128, 1, 128)
     kv = jnp.transpose(jnp.stack([key_states, value_states]), (2, 0, 1, 3))
@@ -414,8 +421,8 @@
         in_specs=[smem] * 5 + [hbm, hbm, vmem, vmem],
         out_specs=[vmem, vmem],
         scratch_shapes=[
-            pltpu.VMEM((n_head * rows, HD), BF16),
-            pltpu.VMEM((n_head * rows, HD), BF16),
+            pltpu.VMEM((span, group, HD), BF16),
+            pltpu.VMEM((span, group, HD), BF16),
             pltpu.VMEM((2, n_head * rows // 128, 1, 128), F32),
             pltpu.VMEM((2, span + 2 * BLK, HD), BF16),
             pltpu.VMEM((2, G * BLK, HD), BF16),
@@ -441,7 +448,7 @@
             collective_id=0, has_side_effects=True, vmem_limit_bytes=60 << 20
         ),
         name="fused",
-    )(jnp.maximum(pick, 0), pos, back, bias, share, by_head(queries), by_head(output_grad), kv, ld)
+    )(jnp.maximum(pick, 0), pos, back, bias, share, queries, output_grad, kv, ld)
 
     query_grad = jnp.transpose(
         dq_all.reshape(n_head, toks, group, HD), (1, 0, 2, 3)

time: 171 us -> 160 us (0.936); the launches traced: 169 us -> 160 us
  local copies, waits for them, and re-layouts: 15.7 us -> 9.92 us
  Pallas kernels: 145 us -> 142 us
    reshape x1 -> x0, local copies, waits for them, and re-layouts: 4.76 us -> none  [by_head(): jnp.transpose(x.reshape(toks, n_head, group, HD), (1, 0, 2, 3))]
    pallas_call x1, Pallas kernels: 145 us -> 142 us  [per_device(): pl.pallas_call(functools.partial(fused, n_seq, n_head, most, blocks), out...]
    unnamed x17 -> x15, local copies, waits for them, and re-layouts: 3.56 us -> 3.41 us
where the time goes in v3:
time: 160 us
  Pallas kernels  142 us (89%)
  local copies, waits for them, and re-layouts  9.92 us (6%)
  other arithmetic  7.48 us (5%)
    pallas_call x1, Pallas kernels, per_device(): pl.pallas_call(functools.partial(fused, n_seq, n_head, most, blocks), out...  142 us
    reduce_sum x1, other arithmetic, per_device(): delta = jnp.sum(output_grad.astype(F32) * outputs.astype(F32), axis=-1)  3.73 us
    reshape x1, local copies, waits for them, and re-layouts, per_device(): query_grad = jnp.transpose(dq_all.reshape(n_head, toks, group, HD), (1, 0...  3.54 us
    unnamed x15, local copies, waits for them, and re-layouts  3.41 us

profile of v3, /device:TPU:0, one launch (start us, length us, event | category | flops | bytes accessed | tf_op | source)
XLA Modules:
  0.0 160.3 jit_solution(8237669904294335174)
XLA Ops:
  0.7 0.8 copy.51
  1.5 0.1 copy.52
  1.6 0.6 convert_reduce_fusion
  2.3 0.8 copy.54
  3.2 0.1 select_reduce_fusion.1
  3.3 0.1 copy.55
  3.4 0.1 sub.13
  3.5 0.5 broadcast_maximum_fusion.pick
  4.0 0.6 fusion.2.share
  4.6 0.1 copy.66
  4.7 0.2 add_reduce_fusion
  4.9 0.6 select_reduce_fusion.back
  5.6 0.1 fusion.3
  5.8 0.6 select_n.25.bias
  6.4 3.7 %multiply_reduce_fusion = f32[288,32]{1,0:T(8,128)S(1)} fusion(bf16[288,32,128]{2,1,0:T(8,128)(2,1)} %param.11, bf16[288,32,128]{2,1,0:T(8,128)(2,1)} %g_in.1), kind=kLoop, calls=%fused_computation | loop fusion | flops 4709376 | bytes 4755456 | tf_op jit(solution)/shard_map/reduce_sum | solution.py:368
  10.1 0.1 copy.60
  10.3 0.1 copy_bitcast_fusion.1
  10.4 0.9 maximum_bitcast_fusion.kv_in
  11.2 0.4 copy.61
  11.6 1.2 reshape.88.ld_in
  12.8 142.1 %fused.1 = (bf16[4,2304,128]{2,1,0:T(8,128)(2,1)}, bf16[4,2,288,128]{3,2,1,0:T(8,128)(2,1)}) custom-call(s32[32]{0:T(128)} %broadcast_maximum_fusion.pick, s32[27]{0:T(128)} %copy-done.4, s32[32]{0:T(128)} %select_reduce_fusion.back, f32[54]{0:T(128)} %select_n.25.bias, f32[9,32]{1,0:T(8,128)} %fusion.2.share, bf16[288,32,128]{2,1,0:T(8,128)(2,1)} %q_in.1, ...), custom_call_target="tpu_custom_call" | custom-call | tf_op jit(solution)/shard_map/fused/pallas_call | solution.py:415
  154.9 3.5 %copy_bitcast_fusion = bf16[288,32,128]{2,1,0:T(8,128)(2,1)} fusion(bf16[4,2304,128]{2,1,0:T(8,128)(2,1)} %get-tuple-element.5), kind=kLoop, calls=%fused_computation.1 | loop fusion | bytes 4718592 | tf_op jit(solution)/shard_map/reshape | solution.py:455
  158.5 0.9 copy.65
  159.4 0.9 copy.64
  (24 shorter events, 0.5 us)
Async XLA Ops:
  4.9 5.2 %copy-start.4 = (s32[27]{0:T(128)}, s32[27]{0:T(128)S(1)}, u32[]{:S(2)}) copy-start(s32[27]{0:T(128)S(1)} %get-tuple-element.23.pos) | copy-start | bytes 328
  6.4 3.9 %copy-start.3 = (f32[288,32]{0,1:T(8,128)S(1)}, f32[288,32]{0,1:T(8,128)}, u32[]{:S(2)}) copy-start(f32[288,32]{0,1:T(8,128)} %param.13) | copy-start | bytes 110596
  6.4 3.9 %copy-start.1 = (bf16[288,4,128]{2,1,0:T(4,128)(2,1)S(1)}, bf16[288,4,128]{2,1,0:T(4,128)(2,1)}, u32[]{:S(2)}) copy-start(bf16[288,4,128]{2,1,0:T(4,128)(2,1)} %param.10) | copy-start | bytes 884740
  6.4 3.9 %copy-start.2 = (bf16[288,4,128]{2,1,0:T(4,128)(2,1)S(1)}, bf16[288,4,128]{2,1,0:T(4,128)(2,1)}, u32[]{:S(2)}) copy-start(bf16[288,4,128]{2,1,0:T(4,128)(2,1)} %param.9) | copy-start | bytes 884740
  154.9 3.5 %copy-start = (bf16[4,2,288,128]{3,2,1,0:T(8,128)(2,1)S(1)}, bf16[4,2,288,128]{3,2,1,0:T(8,128)(2,1)}, u32[]{:S(2)}) copy-start(bf16[4,2,288,128]{3,2,1,0:T(8,128)(2,1)} %get-tuple-element.6) | copy-start | bytes 1769476

commit v4 on v3

--- a/solution.py
+++ b/solution.py
@@ -87,7 +87,6 @@
         base = lax.rem(head + 2 * (d // 2), n_head)
         return base + (1 - 2 * lax.rem(base, 2)) if d % 2 else base
 
-    mine = pl.ds(pl.multiple_of(head * rows, rows), rows)
     here = pl.ds(pl.multiple_of(head * toks, toks), toks)
     q_to = q_all.at[here]
     g_to = g_all.at[here]
@@ -213,11 +212,12 @@
             dq_acc[b] = dq + more
         else:
             total = dq_acc[b] + dq + more
-            dq_all[pl.ds(pl.multiple_of(b * step, step), step), :] = (total.T * scaling).astype(BF16)
+            dq_all[pl.ds(at, BLK)] = (total.T * scaling).astype(BF16).reshape(BLK, group, HD)
 
     def far(i, fresh):
         b = order(i)
         q, g, lse, delta = operands(b)
+        at = pl.multiple_of(b * BLK, BLK)
         found = [rand[pos[b * RND + j]] for j in range(RND)]
         k = jnp.concatenate([f[0] for f in found], axis=0)
         v = jnp.concatenate([f[1] for f in found], axis=0)
@@ -230,7 +230,7 @@
             dq_acc[b] = dq
         else:
             total = dq_acc[b] + dq
-            dq_all[pl.ds(pl.multiple_of(b * step, step), step), :] = (total.T * scaling).astype(BF16)
+            dq_all[pl.ds(at, BLK)] = (total.T * scaling).astype(BF16).reshape(BLK, group, HD)
 
     early = span // 2 // BLK
     loop(0, early, lambda i: near(i, True))
@@ -262,8 +262,8 @@
 
     def dq_copy(d):
         peer = partner(d)
-        src = dq_all.at[pl.ds(pl.multiple_of(peer * rows, rows), rows), :]
-        return remote(src, dq_out.at[head], hs.at[4, d], hr.at[4, d], head=peer)
+        src = dq_all.at[pl.ds(pl.multiple_of(peer * toks, toks), toks)]
+        return remote(src, heads_of(dq_out, head), hs.at[4, d], hr.at[4, d], head=peer)
 
     def kv_copy(d):
         peer = partner(d)
@@ -275,7 +275,7 @@
 
     down_grad = remote(halo_part.at[0], halo.at[0], ns.at[2], nr.at[2], seq=down)
     up_grad = remote(halo_part.at[1], halo.at[1], ns.at[3], nr.at[3], seq=up)
-    own_dq = pltpu.make_async_copy(dq_all.at[mine, :], dq_out.at[head], ls.at[4])
+    own_dq = pltpu.make_async_copy(dq_all.at[here], heads_of(dq_out, head), ls.at[4])
     for d in list(range(2, n_head)) + [1]:
         dq_copy(d).start()
     own_dq.start()
@@ -412,14 +412,14 @@
     )
     slots = n_seq * most
     step = BLK * group
-    dq_all, kv_all = pl.pallas_call(
+    query_grad, kv_all = pl.pallas_call(
         functools.partial(fused, n_seq, n_head, most, blocks),
         out_shape=[
-            jax.ShapeDtypeStruct((n_head, rows, HD), BF16),
+            jax.ShapeDtypeStruct((toks, heads, HD), BF16),
             jax.ShapeDtypeStruct((n_head, 2, toks, HD), BF16),
         ],
         in_specs=[smem] * 5 + [hbm, hbm, vmem, vmem],
-        out_specs=[vmem, vmem],
+        out_specs=[hbm, vmem],
         scratch_shapes=[
             pltpu.VMEM((span, group, HD), BF16),
             pltpu.VMEM((span, group, HD), BF16),
@@ -432,7 +432,7 @@
             pltpu.VMEM((2, span + 2 * BLK, HD), F32),
             pltpu.VMEM((2, G * BLK, HD), F32),
             pltpu.VMEM((blocks, HD, step), F32),
-            pltpu.VMEM((n_head * rows, HD), BF16),
+            pltpu.VMEM((span, group, HD), BF16),
             pltpu.VMEM((per_row, 2, BLK, HD), BF16),
             pltpu.VMEM((slots, 2, BLK, HD), BF16),
             pltpu.VMEM((2, 2, BLK, HD), BF16),
@@ -450,9 +450,6 @@
         name="fused",
     )(jnp.maximum(pick, 0), pos, back, bias, share, queries, output_grad, kv, ld)
 
-    query_grad = jnp.transpose(
-        dq_all.reshape(n_head, toks, group, HD), (1, 0, 2, 3)
-    ).reshape(toks, heads, HD)
     key_grad = jnp.transpose(kv_all[:, 0], (1, 0, 2))
     value_grad = jnp.transpose(kv_all[:, 1], (1, 0, 2))
     return query_grad, key_grad, value_grad

time: 160 us -> 159 us (level)
    reshape x1 -> x0, local copies, waits for them, and re-layouts: 3.54 us -> none  [per_device(): query_grad = jnp.transpose(dq_all.reshape(n_head, toks, group, HD), (1, 0...]
    unnamed x15 -> x16, local copies, waits for them, and re-layouts: 3.41 us -> 4.81 us
where the time goes in v4:
time: 159 us
  Pallas kernels  141 us (89%)
  local copies, waits for them, and re-layouts  8.99 us (6%)
  other arithmetic  7.48 us (5%)
    pallas_call x1, Pallas kernels, per_device(): pl.pallas_call(functools.partial(fused, n_seq, n_head, most, blocks), out...  141 us
    unnamed x16, local copies, waits for them, and re-layouts  4.81 us
    reduce_sum x1, other arithmetic, per_device(): delta = jnp.sum(output_grad.astype(F32) * outputs.astype(F32), axis=-1)  3.73 us

profile of v4, /device:TPU:0, one launch (start us, length us, event | category | flops | bytes accessed | tf_op | source)
XLA Modules:
  0.0 158.6 jit_solution(6693717232584959541)
XLA Ops:
  0.7 0.8 copy.47
  1.5 0.1 copy.48
  1.6 0.6 convert_reduce_fusion
  2.3 0.8 copy.50
  3.2 0.1 select_reduce_fusion.1
  3.3 0.1 copy.51
  3.4 0.1 sub.13
  3.5 0.5 broadcast_maximum_fusion.pick
  4.0 0.6 fusion.2.share
  4.6 0.1 copy.61
  4.7 0.2 add_reduce_fusion
  4.9 0.6 select_reduce_fusion.back
  5.6 0.1 fusion.3
  5.8 0.6 select_n.25.bias
  6.4 3.7 %multiply_reduce_fusion = f32[288,32]{1,0:T(8,128)S(1)} fusion(bf16[288,32,128]{2,1,0:T(8,128)(2,1)} %param.11, bf16[288,32,128]{2,1,0:T(8,128)(2,1)} %g_in.1), kind=kLoop, calls=%fused_computation | loop fusion | flops 4709376 | bytes 4755456 | tf_op jit(solution)/shard_map/reduce_sum | solution.py:368
  10.1 0.1 copy.56
  10.4 0.9 maximum_bitcast_fusion.kv_in
  11.2 0.4 copy.57
  11.6 1.2 reshape.80.ld_in
  12.8 141.3 %fused.1 = (bf16[288,32,128]{2,1,0:T(8,128)(2,1)}, bf16[4,2,288,128]{3,2,1,0:T(8,128)(2,1)}) custom-call(s32[32]{0:T(128)} %broadcast_maximum_fusion.pick, s32[27]{0:T(128)} %copy-done.4, s32[32]{0:T(128)} %select_reduce_fusion.back, f32[54]{0:T(128)} %select_n.25.bias, f32[9,32]{1,0:T(8,128)} %fusion.2.share, bf16[288,32,128]{2,1,0:T(8,128)(2,1)} %q_in.1, ...), custom_call_target="tpu_custom_call" | custom-call | tf_op jit(solution)/shard_map/fused/pallas_call | solution.py:415
  154.2 1.2 slice_bitcast_fusion
  155.4 0.9 copy.60
  156.3 0.9 copy.59
  157.2 1.4 copy.65
  (24 shorter events, 0.5 us)
Async XLA Ops:
  4.9 5.2 %copy-start.4 = (s32[27]{0:T(128)}, s32[27]{0:T(128)S(1)}, u32[]{:S(2)}) copy-start(s32[27]{0:T(128)S(1)} %get-tuple-element.23.pos) | copy-start | bytes 328
  6.4 3.9 %copy-start.3 = (f32[288,32]{0,1:T(8,128)S(1)}, f32[288,32]{0,1:T(8,128)}, u32[]{:S(2)}) copy-start(f32[288,32]{0,1:T(8,128)} %param.13) | copy-start | bytes 110596
  6.4 3.9 %copy-start.1 = (bf16[288,4,128]{2,1,0:T(4,128)(2,1)S(1)}, bf16[288,4,128]{2,1,0:T(4,128)(2,1)}, u32[]{:S(2)}) copy-start(bf16[288,4,128]{2,1,0:T(4,128)(2,1)} %param.10) | copy-start | bytes 884740
  6.4 3.9 %copy-start.2 = (bf16[288,4,128]{2,1,0:T(4,128)(2,1)S(1)}, bf16[288,4,128]{2,1,0:T(4,128)(2,1)}, u32[]{:S(2)}) copy-start(bf16[288,4,128]{2,1,0:T(4,128)(2,1)} %param.9) | copy-start | bytes 884740
  154.2 3.0 %copy-start = (bf16[288,32,128]{2,1,0:T(8,128)(2,1)S(1)}, bf16[288,32,128]{2,1,0:T(8,128)(2,1)}, u32[]{:S(2)}) copy-start(bf16[288,32,128]{2,1,0:T(8,128)(2,1)} %get-tuple-element.33) | copy-start | bytes 7077892
